TPU v7x, 256 devices: a whole 4x4x8 slice. The times are simulated.
256 devices in a mesh: wide: 64 (over z, y, core), narrow: 4 (over x).
Axes of the slice: x: 4, y: 4, z: 8, core: 2. Of those that a mesh axis runs over, the one named last changes fastest.
Arguments:
- stored_amps: float32 [1024, 16384], P('wide', 'narrow'), may hold values from -6 to 6
- integrals: float32 [16384, 16384], P('narrow', 'wide'), may hold values from -0.046875 to 0.046875
- pair_counts: int32 [4], replicated, may hold values from 2048 to 4096, as said below
- block_map: int32 [64], replicated, may hold values from 0 to 63, each once
Outputs:
- cycle_out: float32 [1024, 16384], P('wide', 'narrow')
Inputs may be any that keep to these rules, and one draw needn't show every extreme that they name: `pair_counts`: each count lies between half of 4096 and 4096; one count equals 4096. `block_map`: a permutation of the indices of wide.
All inputs are finite; a program needn't handle non-finite values.
Results may differ from a plain program's by a relative error of at most 0.000086.
Values sent between devices are 32-bit elements; how exact they have to be, the bound alone decides.
No kernel may reach another device: no remote copies, remote signals or barrier semaphores. Data moves between devices by JAX's collectives and lax.ppermute only.
A program may use at most 64 MiB of HBM per device.

v0:
```python
import jax
import jax.numpy as jnp
from jax import lax
from jax.sharding import PartitionSpec as P

PB = 4096
BR = 8


def true_order(rows_block, block_map, count_wide):
    total = rows_block.shape[0]
    width = rows_block.shape[1]
    slots = total // (count_wide * BR)
    shaped = rows_block.reshape(count_wide, slots, BR, width)
    shaped = jnp.take(shaped, block_map, axis=0)
    return jnp.transpose(shaped, (1, 0, 2, 3)).reshape(total, width)


def on_device(stored_amps, integrals, pair_counts, block_map):
    count_wide = lax.axis_size("wide")
    count_narrow = lax.axis_size("narrow")
    layer = lax.axis_index("narrow")
    width = stored_amps.shape[1]
    columns = layer * width + jnp.arange(width, dtype=jnp.int32)
    owner = columns // PB
    limit = jnp.sum(
        jnp.where(
            owner[:, None] == jnp.arange(4, dtype=jnp.int32)[None, :], pair_counts[None, :], 0
        ),
        axis=1,
    )
    masked = jnp.where((columns % PB < limit)[None, :], stored_amps, jnp.float32(0.0))
    local_cols = integrals.shape[1]
    cycle = jnp.dot(
        lax.all_gather(masked, "wide", axis=0, tiled=True),
        integrals,
        precision=lax.Precision.HIGHEST,
        preferred_element_type=jnp.float32,
    )
    ordered = true_order(cycle, block_map, count_wide)
    moved = lax.all_to_all(ordered, "wide", split_axis=0, concat_axis=1, tiled=True)
    height = moved.shape[0]
    group = local_cols // count_narrow
    moved = moved.reshape(height, count_wide, count_narrow, group)
    moved = jnp.transpose(moved, (0, 2, 1, 3)).reshape(height, count_wide * local_cols)
    cycle_out = lax.psum_scatter(moved, "narrow", scatter_dimension=1, tiled=True)
    return cycle_out


def solution(mesh):
    placed = (P("wide", "narrow"), P("narrow", "wide"), P(), P())
    return jax.shard_map(
        on_device, mesh=mesh, in_specs=placed, out_specs=P("wide", "narrow"), check_vma=False
    )
```

profile of v0, /device:TPU:1, one launch (start us, length us, event | category | flops | bytes accessed | tf_op | source)
XLA Modules:
  0.0 200.3 jit_solution(17723670310562345288)
XLA Ops:
  6.5 0.0 all-gather.2.cloned.1.call-start
  6.6 0.8 select_reduce_fusion
  7.4 1.7 broadcast_select_fusion
  9.0 0.0 all-gather.2.cloned.1.call-update
  9.1 0.0 reduce-scatter.2.cloned.1.call-start
  9.1 0.7 compare_select_fusion
  9.8 0.7 compare_and_fusion
  10.4 103.9 %all-gather.2.cloned.1.call-done = f32[1024,4096]{1,0:T(8,128)} async-done(((f32[16,4096]{1,0:T(8,128)}), f32[1024,4096]{1,0:T(8,128)}) %all-gather.2.cloned.1.call-update) | async-done | bytes 16777232 | tf_op jit(solution)/shard_map/all_gather | solution.py:35
  114.3 16.2 %fusion.6 = f32[1024,256]{1,0:T(8,128)S(1)} fusion(f32[1024,4096]{1,0:T(8,128)} %all-gather.2.cloned.1.call-done, f32[4096,256]{1,0:T(8,128)} %param.5), kind=kOutput, calls=%fused_computation.21 | convolution fusion | flops 12884901888 | bytes 22020096 | tf_op jit(solution)/shard_map/dot_general | solution.py:34
  130.5 0.6 gather_fusion
  131.2 0.1 select_bitcast_fusion
  131.3 0.1 copy.9
  131.4 33.8 %all_to_all.16 = f32[64,16,256]{2,1,0:T(8,128)S(1)} all-to-all(f32[64,16,256]{2,1,0:T(8,128)S(1)} %bitcast.11), channel_id=1, replica_groups=mesh['wide'=64,'narrow'=4] {'wide'}, dimensions={0} | all-to-all | bytes 2097152 | tf_op jit(solution)/shard_map/all_to_all | solution.py:41
  165.2 0.6 copy.10
  165.8 0.9 reshape.59
  166.7 1.7 copy.11
  168.3 3.2 %reshape.60 = f32[16,16384]{1,0:T(8,128)} reshape(f32[16,4,64,64]{3,2,1,0:T(8,128)} %copy.11) | data formatting | bytes 2097152 | tf_op jit(solution)/shard_map/reshape | solution.py:45
  171.5 0.0 reduce-scatter.2.cloned.1.call-update
  171.6 21.9 %reduce-scatter.2.cloned.1.call-done = f32[16,4096]{1,0:T(8,128)} async-done(((f32[16,16384]{1,0:T(8,128)}), f32[16,4096]{1,0:T(8,128)}) %reduce-scatter.2.cloned.1.call-update) | async-done | bytes 262160 | tf_op jit(solution)/shard_map/reduce_scatter | solution.py:46
  (3 shorter events, 0.0 us)
Async XLA Ops:
  6.5 107.8 %all-gather.2.cloned.1.call-start = ((), (), s32[]{:S(2)}) async-start(), calls=%async_computation.2 | async-start | bytes 17039360 | tf_op jit(solution)/shard_map/all_gather | solution.py:35
  9.1 184.4 %reduce-scatter.2.cloned.1.call-start = ((), (), s32[]{:S(2)}) async-start(), calls=%async_computation.3 | async-start | bytes 1310720 | tf_op jit(solution)/shard_map/reduce_scatter | solution.py:46
Sparse Core Ops, SparseCore 0:
  10.1 104.1 all-gather.1
  171.7 21.7 reduce-scatter.1
where the time goes:
time: 201 us; the launch traced here: 200 us
  waiting for transfers between devices  126 us (63%)
  blocking collectives  33.8 us (17%)
  matrix products  16.2 us (8%)
  between operations  13.5 us (7%)
  local copies, waits for them, and re-layouts  7.09 us (4%)
  other arithmetic  3.96 us (2%)
    all_gather x1, waiting for transfers between devices, on_device(): lax.all_gather(masked, 'wide', axis=0, tiled=True)  104 us
    all_to_all x1, blocking collectives, on_device(): lax.all_to_all(ordered, 'wide', split_axis=0, concat_axis=1, tiled=True)  33.8 us
    reduce_scatter x1, waiting for transfers between devices, on_device(): lax.psum_scatter(moved, 'narrow', scatter_dimension=1, tiled=True)  21.9 us
    dot_general x1, matrix products, on_device(): jnp.dot(lax.all_gather(masked, 'wide', axis=0, tiled=True), integrals, pr...  16.2 us
  transfers between devices with their start and end apart: 2, of which 2 were waited for; matrix products, arithmetic and copies ran while one was open for 1% of the time, Pallas kernels for 0%

commit v1 on v0

v1 whole, which is shorter than its diff:
```python
import jax
import jax.numpy as jnp
from jax import lax
from jax.sharding import PartitionSpec as P

NZ, NY, NC, NX = 8, 4, 2, 4
BR = 8
G = 64


def wide_pairs(dz, dy, dc=0):
    pairs = []
    for z in range(NZ):
        for y in range(NY):
            for c in range(NC):
                source = (z * NY + y) * NC + c
                target = (((z + dz) % NZ) * NY + (y + dy) % NY) * NC + (c + dc) % NC
                pairs.append((source, target))
    return pairs


def along_z(block, step):
    return lax.ppermute(block, "wide", wide_pairs(step, 0))


def along_y(block, step):
    return lax.ppermute(block, "wide", wide_pairs(0, step))


def other_core(block):
    return lax.ppermute(block, "wide", wide_pairs(0, 0, 1))


def along_x(block, step):
    return lax.ppermute(block, "narrow", [(i, (i + step) % NX) for i in range(NX)])


def on_device(stored_amps, integrals, pair_counts, block_map):
    place = lax.axis_index("wide")
    layer = lax.axis_index("narrow")
    core = place % NC
    my_y = (place // NC) % NY
    my_z = place // (NC * NY)
    width = stored_amps.shape[1]
    half = width // 2

    live = jnp.arange(width, dtype=jnp.int32)[:, None] < pair_counts[layer]
    integrals = jnp.where(live, integrals, jnp.float32(0.0))
    theirs = other_core(integrals)

    top, low = stored_amps[:BR], stored_amps[BR:]

    ya, yb = along_y(low, 1), along_y(low, -1)
    za, zb = along_z(top, 1), along_z(top, -1)
    yc = jnp.concatenate([along_y(ya[:, :half], 1), along_y(yb[:, half:], -1)], axis=1)
    row = jnp.concatenate([low, ya, yb, yc], axis=0)
    first = jnp.concatenate([top, za, zb], axis=0)
    zc, zd = along_z(za, 1), along_z(zb, -1)
    fa, fb = along_y(first, 1), along_y(first, -1)
    ra, rb = along_z(row, 1), along_z(row, -1)
    ze, zf = along_z(zc, 1), along_z(zd, -1)
    zg = jnp.concatenate([along_z(ze[:, :half], 1), along_z(zf[:, half:], -1)], axis=1)
    second = jnp.concatenate([zc, zd, ze, zf, zg], axis=0)
    fc = jnp.concatenate([along_y(fa[:, :half], 1), along_y(fb[:, half:], -1)], axis=1)
    sa, sb = along_y(second, 1), along_y(second, -1)
    rc, rd = along_z(ra, 1), along_z(rb, -1)
    re, rf = along_z(rc, 1), along_z(rd, -1)
    sc = jnp.concatenate([along_y(sa[:, :half], 1), along_y(sb[:, half:], -1)], axis=1)
    rg = jnp.concatenate([along_z(re[:, :half], 1), along_z(rf[:, half:], -1)], axis=1)

    rows = jnp.concatenate(
        [first, second, fa, sa, fb, sb, fc, sc, row, ra, rb, rc, rd, re, rf, rg], axis=0
    )

    def times(held):
        return jnp.dot(
            rows, held, precision=lax.Precision.HIGH, preferred_element_type=jnp.float32
        )

    mine, others = times(integrals), times(theirs)
    even = jnp.where(core == 0, mine, others)
    odd = jnp.where(core == 0, others, mine)
    count = rows.shape[0]
    chunks = jnp.concatenate(
        [even.reshape(count, NX, G), odd.reshape(count, NX, G)], axis=2
    )
    chunks = jnp.transpose(chunks, (1, 0, 2))

    def chunk(step):
        return lax.dynamic_index_in_dim(chunks, (layer + step) % NX, 0, keepdims=False)

    total = chunk(0)
    for step in (1, 3, 2):
        total = total + along_x(chunk(step), step)

    sibling = other_core(total)
    both = jnp.stack([jnp.where(core == 0, total, sibling), jnp.where(core == 0, sibling, total)])
    blocks = both.reshape(NC * (count // BR), BR, 2 * G)

    target = jnp.arange(NZ * NY * NC, dtype=jnp.int32)
    pairs = target.shape[0] // 2
    owner = block_map[2 * (target % pairs) + core]
    slot_z = jnp.array([0, 2, 4, 6, 7, 5, 3, 1], jnp.int32)
    slot_y = jnp.array([0, 2, 3, 1], jnp.int32)
    kz = slot_z[(owner // (NC * NY) - my_z) % NZ]
    ky = slot_y[((owner // NC) % NY - my_y) % NY]
    where_top = ky * NZ + kz
    where_low = NZ * NY + kz * NY + ky
    at = jnp.where(target < pairs, where_top, where_low) + (owner % NC) * (2 * NZ * NY)
    sent = jnp.take(blocks, at, axis=0, mode="clip")
    got = lax.all_to_all(sent, "wide", split_axis=0, concat_axis=0, tiled=True)
    got = got.reshape(NZ * NY, NC, BR, 2 * G)
    return jnp.transpose(got, (1, 2, 0, 3)).reshape(NC * BR, NZ * NY * 2 * G)


def solution(mesh):
    placed = (P("wide", "narrow"), P("narrow", "wide"), P(), P())
    return jax.shard_map(
        on_device, mesh=mesh, in_specs=placed, out_specs=P("wide", "narrow"), check_vma=False
    )
```

time: 201 us -> 164 us (0.82)
  waiting for transfers between devices: 126 us -> 30.3 us
  starting transfers between devices: 0.04 us -> 60.5 us
  local copies, waits for them, and re-layouts: 7.09 us -> 22.7 us
  between operations: 13.5 us -> 0.3 us
  blocking collectives: 33.8 us -> 21.4 us
  matrix products: 16.2 us -> 20.9 us
  other arithmetic: 3.96 us -> 7.38 us
    all_gather x1 -> x0, waiting for transfers between devices: 104 us -> none  [on_device(): lax.all_gather(masked, 'wide', axis=0, tiled=True)]
    ppermute x0 -> x33, starting transfers between devices: none -> 60.5 us  [the longest x16 26.8 us: along_z(): return lax.ppermute(block, 'wide', wide_pairs(step, 0))]
    ppermute x0 -> x33, waiting for transfers between devices: none -> 30.3 us  [the longest x12 13.2 us: along_y(): return lax.ppermute(block, 'wide', wide_pairs(0, step))]
    reduce_scatter x1 -> x0, waiting for transfers between devices: 21.9 us -> none  [on_device(): lax.psum_scatter(moved, 'narrow', scatter_dimension=1, tiled=True)]
    unnamed x0 -> x30, local copies, waits for them, and re-layouts: none -> 17.7 us
    all_to_all x1, blocking collectives: 33.8 us -> 21.4 us  [on_device(): got = lax.all_to_all(sent, 'wide', split_axis=0, concat_axis=0, tiled=True)]
    dot_general x1 -> x2, matrix products: 16.2 us -> 20.9 us  [times(): jnp.dot(rows, held, precision=lax.Precision.HIGH, preferred_element_type=...]
    reshape x2 -> x0, local copies, waits for them, and re-layouts: 4.11 us -> none  [the longest x1 3.23 us: on_device(): jnp.transpose(moved, (0, 2, 1, 3)).reshape(height, count_wide * local_cols)]
  transfers between devices with their start and end apart: 2 -> 33, of which waited for: 2 -> 15; matrix products, arithmetic and copies ran while one was open for 1% -> 23% of each run, Pallas kernels for 0% -> 0%
where the time goes in v1:
time: 164 us
  starting transfers between devices  60.5 us (37%)
  waiting for transfers between devices  30.3 us (18%)
  local copies, waits for them, and re-layouts  22.7 us (14%)
  blocking collectives  21.4 us (13%)
  matrix products  20.9 us (13%)
  other arithmetic  7.38 us (4%)
    ppermute x16, starting transfers between devices, along_z(): return lax.ppermute(block, 'wide', wide_pairs(step, 0))  26.8 us
    all_to_all x1, blocking collectives, on_device(): got = lax.all_to_all(sent, 'wide', split_axis=0, concat_axis=0, tiled=True)  21.4 us
    dot_general x2, matrix products, times(): jnp.dot(rows, held, precision=lax.Precision.HIGH, preferred_element_type=...  20.9 us
    unnamed x30, local copies, waits for them, and re-layouts  17.7 us
    ppermute x12, starting transfers between devices, along_y(): return lax.ppermute(block, 'wide', wide_pairs(0, step))  17.3 us
    ppermute x12, waiting for transfers between devices, along_y(): return lax.ppermute(block, 'wide', wide_pairs(0, step))  13.2 us
    ppermute x2, starting transfers between devices, other_core(): return lax.ppermute(block, 'wide', wide_pairs(0, 0, 1))  12 us
    ppermute x16, waiting for transfers between devices, along_z(): return lax.ppermute(block, 'wide', wide_pairs(step, 0))  11.3 us
  transfers between devices with their start and end apart: 33, of which 15 were waited for; matrix products, arithmetic and copies ran while one was open for 23% of the time, Pallas kernels for 0%

profile of v1, /device:TPU:1, one launch (start us, length us, event | category | flops | bytes accessed | tf_op | source)
XLA Modules:
  0.0 163.5 jit_solution(4598660155578012005)
XLA Ops:
  0.0 1.6 %fusion.18 = (f32[8,4096]{1,0:T(8,128)S(1)}, f32[512,4096]{1,0:T(8,128)}, f32[8,4096]{1,0:T(8,128)S(1)}) fusion(f32[16,4096]{1,0:T(8,128)} %param.6), kind=kLoop, calls=%fused_computation.108 | loop fusion | bytes 655360 | tf_op jit(solution)/shard_map/slice | solution.py:51
  1.7 2.5 %collective-permute-start = (f32[8,4096]{1,0:T(8,128)S(1)}, f32[8,4096]{1,0:T(8,128)S(1)}, u32[]{:S(2)}, u32[]{:S(2)}) collective-permute-start(f32[8,4096]{1,0:T(8,128)S(1)} %get-tuple-element.15), channel_id=1, source_target_pairs={{0,32},{4,36},{8,40},{12,44},{16,48},{20,52},{24,56},{28,60},{32,6... | collective-permute-start | bytes 393224 | tf_op jit(solution)/shard_map/ppermute | solution.py:23
  4.1 3.9 %collective-permute-start.1 = (f32[8,4096]{1,0:T(8,128)S(1)}, f32[8,4096]{1,0:T(8,128)S(1)}, u32[]{:S(2)}, u32[]{:S(2)}) collective-permute-start(f32[8,4096]{1,0:T(8,128)S(1)} %get-tuple-element.15), channel_id=1, source_target_pairs={{0,224},{4,228},{8,232},{12,236},{16,240},{20,244},{24,248},{28,25... | collective-permute-start | bytes 393224 | tf_op jit(solution)/shard_map/ppermute | solution.py:23
  8.1 1.3 collective-permute-start.16
  9.4 1.4 collective-permute-start.17
  10.8 1.2 dynamic_slice.8
  12.7 3.9 %broadcast_select_fusion = f32[4096,256]{1,0:T(8,128)} fusion(f32[4096,256]{1,0:T(8,128)} %param.7, pred[4096]{0:T(1024)(128)(4,1)S(1)} %iota_compare_fusion), kind=kLoop, calls=%fused_computation.2 | loop fusion | flops 1048576 | bytes 8392704 | tf_op jit(solution)/shard_map/jit(_where)/select_n | solution.py:48
  16.6 1.5 collective-permute-start.28
  18.2 2.6 %collective-permute-start.10 = (f32[24,4096]{1,0:T(8,128)S(1)}, f32[24,4096]{1,0:T(8,128)S(1)}, u32[]{:S(2)}, u32[]{:S(2)}) collective-permute-start(f32[24,4096]{1,0:T(8,128)S(1)} %pad_maximum_fusion.1), channel_id=1, source_target_pairs={{0,24},{4,28},{8,0},{12,4},{16,8},{20,12},{24,16},{28,20},{32,56},... | collective-permute-start | bytes 1179656 | tf_op jit(solution)/shard_map/ppermute | solution.py:27
  20.9 2.7 %collective-permute-start.19 = (f32[8,2048]{1,0:T(8,128)S(1)}, f32[8,2048]{1,0:T(8,128)S(1)}, u32[]{:S(2)}, u32[]{:S(2)}) collective-permute-start(f32[8,2048]{1,0:T(8,128)S(1)} %slice.73), channel_id=1, source_target_pairs={{0,24},{4,28},{8,0},{12,4},{16,8},{20,12},{24,16},{28,20},{32,56},... | collective-permute-start | bytes 196616 | tf_op jit(solution)/shard_map/ppermute | solution.py:27
  25.0 6.5 %collective-permute-done.18 = f32[8,2048]{1,0:T(8,128)S(1)} collective-permute-done((f32[8,2048]{1,0:T(8,128)S(1)}, f32[8,2048]{1,0:T(8,128)S(1)}, u32[]{:S(2)}, u32[]{:S(2)}) %collective-permute-start.18) | collective-permute-done | bytes 65568 | tf_op jit(solution)/shard_map/ppermute | solution.py:27
  31.5 2.7 %collective-permute-start.3 = (f32[8,4096]{1,0:T(8,128)S(1)}, f32[8,4096]{1,0:T(8,128)S(1)}, u32[]{:S(2)}, u32[]{:S(2)}) collective-permute-start(f32[8,4096]{1,0:T(8,128)S(1)} %collective-permute-done.1), channel_id=1, source_target_pairs={{0,224},{4,228},{8,232},{12,236},{16,240},{20,244},{24,248},{28,25... | collective-permute-start | bytes 393224 | tf_op jit(solution)/shard_map/ppermute | solution.py:23
  34.2 2.7 %collective-permute-done.2 = f32[8,4096]{1,0:T(8,128)S(1)} collective-permute-done((f32[8,4096]{1,0:T(8,128)S(1)}, f32[8,4096]{1,0:T(8,128)S(1)}, u32[]{:S(2)}, u32[]{:S(2)}) %collective-permute-start.2) | collective-permute-done | bytes 131104 | tf_op jit(solution)/shard_map/ppermute | solution.py:23
  37.6 2.7 %collective-permute-start.5 = (f32[8,4096]{1,0:T(8,128)S(1)}, f32[8,4096]{1,0:T(8,128)S(1)}, u32[]{:S(2)}, u32[]{:S(2)}) collective-permute-start(f32[8,4096]{1,0:T(8,128)S(1)} %collective-permute-done.3), channel_id=1, source_target_pairs={{0,224},{4,228},{8,232},{12,236},{16,240},{20,244},{24,248},{28,25... | collective-permute-start | bytes 393224 | tf_op jit(solution)/shard_map/ppermute | solution.py:23
  40.9 1.0 collective-permute-done.4
  42.2 3.1 %collective-permute-start.7 = (f32[8,2048]{1,0:T(8,128)S(1)}, f32[8,2048]{1,0:T(8,128)S(1)}, u32[]{:S(2)}, u32[]{:S(2)}) collective-permute-start(f32[8,2048]{1,0:T(8,128)S(1)} %slice.67), channel_id=1, source_target_pairs={{0,224},{4,228},{8,232},{12,236},{16,240},{20,244},{24,248},{28,25... | collective-permute-start | bytes 196616 | tf_op jit(solution)/shard_map/ppermute | solution.py:23
  48.0 3.0 %collective-permute-start.21 = (f32[32,4096]{1,0:T(8,128)S(1)}, f32[32,4096]{1,0:T(8,128)S(1)}, u32[]{:S(2)}, u32[]{:S(2)}) collective-permute-start(f32[32,4096]{1,0:T(8,128)S(1)} %maximum_maximum_fusion), channel_id=1, source_target_pairs={{0,224},{4,228},{8,232},{12,236},{16,240},{20,244},{24,248},{28,25... | collective-permute-start | bytes 1572872 | tf_op jit(solution)/shard_map/ppermute | solution.py:23
  51.0 2.7 %collective-permute-start.11 = (f32[40,4096]{1,0:T(8,128)S(1)}, f32[40,4096]{1,0:T(8,128)S(1)}, u32[]{:S(2)}, u32[]{:S(2)}) collective-permute-start(f32[40,4096]{1,0:T(8,128)S(1)} %maximum_dynamic-update-slice_fusion.3), channel_id=1, source_target_pairs={{0,24},{4,28},{8,0},{12,4},{16,8},{20,12},{24,16},{28,20},{32,56},... | collective-permute-start | bytes 1966088 | tf_op jit(solution)/shard_map/ppermute | solution.py:27
  54.5 5.7 %collective-permute-done.9 = f32[40,4096]{1,0:T(8,128)S(1)} collective-permute-done((f32[40,4096]{1,0:T(8,128)S(1)}, f32[40,4096]{1,0:T(8,128)S(1)}, u32[]{:S(2)}, u32[]{:S(2)}) %collective-permute-start.9) | collective-permute-done | bytes 655392 | tf_op jit(solution)/shard_map/ppermute | solution.py:27
  60.2 0.9 constant_dynamic-update-slice_fusion.16
  61.9 2.7 %collective-permute-start.13 = (f32[24,2048]{1,0:T(8,128)S(1)}, f32[24,2048]{1,0:T(8,128)S(1)}, u32[]{:S(2)}, u32[]{:S(2)}) collective-permute-start(f32[24,2048]{1,0:T(8,128)S(1)} %slice.69), channel_id=1, source_target_pairs={{0,24},{4,28},{8,0},{12,4},{16,8},{20,12},{24,16},{28,20},{32,56},... | collective-permute-start | bytes 589832 | tf_op jit(solution)/shard_map/ppermute | solution.py:27
  65.0 2.4 %collective-permute-start.23 = (f32[32,4096]{1,0:T(8,128)S(1)}, f32[32,4096]{1,0:T(8,128)S(1)}, u32[]{:S(2)}, u32[]{:S(2)}) collective-permute-start(f32[32,4096]{1,0:T(8,128)S(1)} %collective-permute-done.21), channel_id=1, source_target_pairs={{0,224},{4,228},{8,232},{12,236},{16,240},{20,244},{24,248},{28,25... | collective-permute-start | bytes 1572872 | tf_op jit(solution)/shard_map/ppermute | solution.py:23
  67.4 0.9 constant_dynamic-update-slice_fusion.14
  68.4 1.0 collective-permute-done.13
  69.4 3.4 %collective-permute-start.15 = (f32[40,2048]{1,0:T(8,128)S(1)}, f32[40,2048]{1,0:T(8,128)S(1)}, u32[]{:S(2)}, u32[]{:S(2)}) collective-permute-start(f32[40,2048]{1,0:T(8,128)S(1)} %slice.71), channel_id=1, source_target_pairs={{0,24},{4,28},{8,0},{12,4},{16,8},{20,12},{24,16},{28,20},{32,56},... | collective-permute-start | bytes 983048 | tf_op jit(solution)/shard_map/ppermute | solution.py:27
  73.9 3.0 %collective-permute-start.25 = (f32[32,4096]{1,0:T(8,128)S(1)}, f32[32,4096]{1,0:T(8,128)S(1)}, u32[]{:S(2)}, u32[]{:S(2)}) collective-permute-start(f32[32,4096]{1,0:T(8,128)S(1)} %collective-permute-done.23), channel_id=1, source_target_pairs={{0,224},{4,228},{8,232},{12,236},{16,240},{20,244},{24,248},{28,25... | collective-permute-start | bytes 1572872 | tf_op jit(solution)/shard_map/ppermute | solution.py:23
  76.9 0.9 maximum_dynamic-update-slice_fusion
  81.0 0.9 constant_dynamic-update-slice_fusion.9
  81.9 0.8 constant_dynamic-update-slice_fusion.8
  82.7 0.8 constant_dynamic-update-slice_fusion.7
  83.6 0.8 constant_dynamic-update-slice_fusion.6
  84.4 1.8 %collective-permute-done.24 = f32[32,4096]{1,0:T(8,128)S(1)} collective-permute-done((f32[32,4096]{1,0:T(8,128)S(1)}, f32[32,4096]{1,0:T(8,128)S(1)}, u32[]{:S(2)}, u32[]{:S(2)}) %collective-permute-start.24) | collective-permute-done | bytes 524320 | tf_op jit(solution)/shard_map/ppermute | solution.py:23
  86.3 3.2 %collective-permute-start.27 = (f32[32,2048]{1,0:T(8,128)S(1)}, f32[32,2048]{1,0:T(8,128)S(1)}, u32[]{:S(2)}, u32[]{:S(2)}) collective-permute-start(f32[32,2048]{1,0:T(8,128)S(1)} %slice.75), channel_id=1, source_target_pairs={{0,224},{4,228},{8,232},{12,236},{16,240},{20,244},{24,248},{28,25... | collective-permute-start | bytes 786440 | tf_op jit(solution)/shard_map/ppermute | solution.py:23
  89.5 0.8 constant_dynamic-update-slice_fusion.5
  90.4 0.9 constant_dynamic-update-slice_fusion.4
  91.3 4.6 %collective-permute-done.26 = f32[32,2048]{1,0:T(8,128)S(1)} collective-permute-done((f32[32,2048]{1,0:T(8,128)S(1)}, f32[32,2048]{1,0:T(8,128)S(1)}, u32[]{:S(2)}, u32[]{:S(2)}) %collective-permute-start.26) | collective-permute-done | bytes 262176 | tf_op jit(solution)/shard_map/ppermute | solution.py:23
  96.4 0.9 maximum_dynamic-update-slice_fusion.1
  97.3 10.6 %fusion.19 = f32[512,256]{0,1:T(8,128)S(1)} fusion(f32[512,4096]{1,0:T(8,128)} %maximum_dynamic-update-slice_fusion.1, f32[4096,256]{1,0:T(8,128)} %broadcast_select_fusion), kind=kOutput, calls=%fused_computation.109 | convolution fusion | flops 3221225472 | bytes 13107200 | tf_op jit(solution)/shard_map/dot_general | solution.py:76
  107.9 10.3 %broadcast_select_fusion.1 = (f32[512,256]{0,1:T(8,128)S(1)}, f32[512,256]{0,1:T(8,128)S(1)}) fusion(f32[512,256]{0,1:T(8,128)S(1)} %fusion.19, pred[]{:T(512)S(6)} %eq.19, f32[512,4096]{1,0:T(8,128)S(1)} %copy-done.1, f32[4096,256]{1,0:T(8,128)} %collective-permute-done.28), kind=kOutput, calls=%fused_computation.28 | convolution fusion | flops 3221487616 | bytes 14155777 | tf_op jit(solution)/shard_map/dot_general | solution.py:76
  118.5 1.3 collective-permute-start.29
  119.9 1.5 collective-permute-start.30
  121.6 1.6 collective-permute-start.31
  124.1 0.9 collective-permute-done.29
  125.2 3.6 %collective-permute-done.31 = f32[512,128]{1,0:T(8,128)S(1)} collective-permute-done((f32[512,128]{1,0:T(8,128)S(1)}, f32[512,128]{1,0:T(8,128)S(1)}, u32[]{:S(2)}, u32[]{:S(2)}) %collective-permute-start.31) | collective-permute-done | bytes 262176 | tf_op jit(solution)/shard_map/ppermute | solution.py:35
  128.8 10.5 %collective-permute-start.32 = (f32[512,128]{1,0:T(8,128)S(1)}, f32[512,128]{1,0:T(8,128)S(1)}, u32[]{:S(2)}, u32[]{:S(2)}) collective-permute-start(f32[512,128]{1,0:T(8,128)S(1)} %fusion.5), channel_id=1, source_target_pairs={{0,4},{4,0},{8,12},{12,8},{16,20},{20,16},{24,28},{28,24},{32,36},... | collective-permute-start | bytes 786440 | tf_op jit(solution)/shard_map/ppermute | solution.py:31
  139.4 1.1 collective-permute-done.32
  141.2 21.4 %all_to_all.5 = f32[64,8,128]{2,1,0:T(8,128)S(1)} all-to-all(f32[64,8,128]{2,1,0:T(8,128)S(1)} %gather_fusion.1), channel_id=1, replica_groups=mesh['wide'=64,'narrow'=4] {'wide'}, dimensions={0} | all-to-all | bytes 524288 | tf_op jit(solution)/shard_map/all_to_all | solution.py:111
  162.7 0.9 copy.19
  (86 shorter events, 16.1 us)
Async XLA Ops:
  0.0 123.2 %copy-start = (s32[64]{0:T(128)S(1)}, s32[64]{0:T(128)}, u32[]{:S(2)}) copy-start(s32[64]{0:T(128)} %param.9) | copy-start | bytes 772
  1.7 16.4 %collective-permute-start = (f32[8,4096]{1,0:T(8,128)S(1)}, f32[8,4096]{1,0:T(8,128)S(1)}, u32[]{:S(2)}, u32[]{:S(2)}) collective-permute-start(f32[8,4096]{1,0:T(8,128)S(1)} %get-tuple-element.15), channel_id=1, source_target_pairs={{0,32},{4,36},{8,40},{12,44},{16,48},{20,52},{24,56},{28,60},{32,6... | collective-permute-start | bytes 393224 | tf_op jit(solution)/shard_map/ppermute | solution.py:23
  4.1 13.9 %collective-permute-start.1 = (f32[8,4096]{1,0:T(8,128)S(1)}, f32[8,4096]{1,0:T(8,128)S(1)}, u32[]{:S(2)}, u32[]{:S(2)}) collective-permute-start(f32[8,4096]{1,0:T(8,128)S(1)} %get-tuple-element.15), channel_id=1, source_target_pairs={{0,224},{4,228},{8,232},{12,236},{16,240},{20,244},{24,248},{28,25... | collective-permute-start | bytes 393224 | tf_op jit(solution)/shard_map/ppermute | solution.py:23
  8.1 12.8 %collective-permute-start.16 = (f32[8,4096]{1,0:T(8,128)S(1)}, f32[8,4096]{1,0:T(8,128)S(1)}, u32[]{:S(2)}, u32[]{:S(2)}) collective-permute-start(f32[8,4096]{1,0:T(8,128)S(1)} %get-tuple-element.13), channel_id=1, source_target_pairs={{0,8},{4,12},{8,16},{12,20},{16,24},{20,28},{24,0},{28,4},{32,40},... | collective-permute-start | bytes 393224 | tf_op jit(solution)/shard_map/ppermute | solution.py:27
  9.4 11.6 %collective-permute-start.17 = (f32[8,4096]{1,0:T(8,128)S(1)}, f32[8,4096]{1,0:T(8,128)S(1)}, u32[]{:S(2)}, u32[]{:S(2)}) collective-permute-start(f32[8,4096]{1,0:T(8,128)S(1)} %get-tuple-element.13), channel_id=1, source_target_pairs={{0,24},{4,28},{8,0},{12,4},{16,8},{20,12},{24,16},{28,20},{32,56},... | collective-permute-start | bytes 393224 | tf_op jit(solution)/shard_map/ppermute | solution.py:27
  16.6 61.2 %copy-start.2 = (f32[16,4096]{1,0:T(8,128)S(1)}, f32[16,4096]{1,0:T(8,128)}, u32[]{:S(2)}) copy-start(f32[16,4096]{1,0:T(8,128)} %param.6) | copy-start | bytes 786436
  16.6 91.4 %collective-permute-start.28 = (f32[4096,256]{1,0:T(8,128)}, f32[4096,256]{1,0:T(8,128)}, u32[]{:S(2)}, u32[]{:S(2)}) collective-permute-start(f32[4096,256]{1,0:T(8,128)} %broadcast_select_fusion), channel_id=1, source_target_pairs={{0,4},{4,0},{8,12},{12,8},{16,20},{20,16},{24,28},{28,24},{32,36},... | collective-permute-start | bytes 12582920 | tf_op jit(solution)/shard_map/ppermute | solution.py:31
  18.1 30.0 %collective-permute-start.8 = (f32[24,4096]{1,0:T(8,128)S(1)}, f32[24,4096]{1,0:T(8,128)S(1)}, u32[]{:S(2)}, u32[]{:S(2)}) collective-permute-start(f32[24,4096]{1,0:T(8,128)S(1)} %pad_maximum_fusion.1), channel_id=1, source_target_pairs={{0,8},{4,12},{8,16},{12,20},{16,24},{20,28},{24,0},{28,4},{32,40},... | collective-permute-start | bytes 1179656 | tf_op jit(solution)/shard_map/ppermute | solution.py:27
  18.2 32.8 %collective-permute-start.10 = (f32[24,4096]{1,0:T(8,128)S(1)}, f32[24,4096]{1,0:T(8,128)S(1)}, u32[]{:S(2)}, u32[]{:S(2)}) collective-permute-start(f32[24,4096]{1,0:T(8,128)S(1)} %pad_maximum_fusion.1), channel_id=1, source_target_pairs={{0,24},{4,28},{8,0},{12,4},{16,8},{20,12},{24,16},{28,20},{32,56},... | collective-permute-start | bytes 1179656 | tf_op jit(solution)/shard_map/ppermute | solution.py:27
  20.8 10.7 %collective-permute-start.18 = (f32[8,2048]{1,0:T(8,128)S(1)}, f32[8,2048]{1,0:T(8,128)S(1)}, u32[]{:S(2)}, u32[]{:S(2)}) collective-permute-start(f32[8,2048]{1,0:T(8,128)S(1)} %slice.72), channel_id=1, source_target_pairs={{0,8},{4,12},{8,16},{12,20},{16,24},{20,28},{24,0},{28,4},{32,40},... | collective-permute-start | bytes 196616 | tf_op jit(solution)/shard_map/ppermute | solution.py:27
  20.9 10.6 %collective-permute-start.19 = (f32[8,2048]{1,0:T(8,128)S(1)}, f32[8,2048]{1,0:T(8,128)S(1)}, u32[]{:S(2)}, u32[]{:S(2)}) collective-permute-start(f32[8,2048]{1,0:T(8,128)S(1)} %slice.73), channel_id=1, source_target_pairs={{0,24},{4,28},{8,0},{12,4},{16,8},{20,12},{24,16},{28,20},{32,56},... | collective-permute-start | bytes 196616 | tf_op jit(solution)/shard_map/ppermute | solution.py:27
  31.5 5.4 %collective-permute-start.2 = (f32[8,4096]{1,0:T(8,128)S(1)}, f32[8,4096]{1,0:T(8,128)S(1)}, u32[]{:S(2)}, u32[]{:S(2)}) collective-permute-start(f32[8,4096]{1,0:T(8,128)S(1)} %collective-permute-done), channel_id=1, source_target_pairs={{0,32},{4,36},{8,40},{12,44},{16,48},{20,52},{24,56},{28,60},{32,6... | collective-permute-start | bytes 393224 | tf_op jit(solution)/shard_map/ppermute | solution.py:23
  31.5 6.1 %collective-permute-start.3 = (f32[8,4096]{1,0:T(8,128)S(1)}, f32[8,4096]{1,0:T(8,128)S(1)}, u32[]{:S(2)}, u32[]{:S(2)}) collective-permute-start(f32[8,4096]{1,0:T(8,128)S(1)} %collective-permute-done.1), channel_id=1, source_target_pairs={{0,224},{4,228},{8,232},{12,236},{16,240},{20,244},{24,248},{28,25... | collective-permute-start | bytes 393224 | tf_op jit(solution)/shard_map/ppermute | solution.py:23
  36.9 5.0 %collective-permute-start.4 = (f32[8,4096]{1,0:T(8,128)S(1)}, f32[8,4096]{1,0:T(8,128)S(1)}, u32[]{:S(2)}, u32[]{:S(2)}) collective-permute-start(f32[8,4096]{1,0:T(8,128)S(1)} %collective-permute-done.2), channel_id=1, source_target_pairs={{0,32},{4,36},{8,40},{12,44},{16,48},{20,52},{24,56},{28,60},{32,6... | collective-permute-start | bytes 393224 | tf_op jit(solution)/shard_map/ppermute | solution.py:23
  37.6 4.6 %collective-permute-start.5 = (f32[8,4096]{1,0:T(8,128)S(1)}, f32[8,4096]{1,0:T(8,128)S(1)}, u32[]{:S(2)}, u32[]{:S(2)}) collective-permute-start(f32[8,4096]{1,0:T(8,128)S(1)} %collective-permute-done.3), channel_id=1, source_target_pairs={{0,224},{4,228},{8,232},{12,236},{16,240},{20,244},{24,248},{28,25... | collective-permute-start | bytes 393224 | tf_op jit(solution)/shard_map/ppermute | solution.py:23
  42.0 4.7 %collective-permute-start.6 = (f32[8,2048]{1,0:T(8,128)S(1)}, f32[8,2048]{1,0:T(8,128)S(1)}, u32[]{:S(2)}, u32[]{:S(2)}) collective-permute-start(f32[8,2048]{1,0:T(8,128)S(1)} %slice.66), channel_id=1, source_target_pairs={{0,32},{4,36},{8,40},{12,44},{16,48},{20,52},{24,56},{28,60},{32,6... | collective-permute-start | bytes 196616 | tf_op jit(solution)/shard_map/ppermute | solution.py:23
  42.2 4.4 %collective-permute-start.7 = (f32[8,2048]{1,0:T(8,128)S(1)}, f32[8,2048]{1,0:T(8,128)S(1)}, u32[]{:S(2)}, u32[]{:S(2)}) collective-permute-start(f32[8,2048]{1,0:T(8,128)S(1)} %slice.67), channel_id=1, source_target_pairs={{0,224},{4,228},{8,232},{12,236},{16,240},{20,244},{24,248},{28,25... | collective-permute-start | bytes 196616 | tf_op jit(solution)/shard_map/ppermute | solution.py:23
  46.6 15.3 %collective-permute-start.20 = (f32[32,4096]{1,0:T(8,128)S(1)}, f32[32,4096]{1,0:T(8,128)S(1)}, u32[]{:S(2)}, u32[]{:S(2)}) collective-permute-start(f32[32,4096]{1,0:T(8,128)S(1)} %maximum_maximum_fusion), channel_id=1, source_target_pairs={{0,32},{4,36},{8,40},{12,44},{16,48},{20,52},{24,56},{28,60},{32,6... | collective-permute-start | bytes 1572872 | tf_op jit(solution)/shard_map/ppermute | solution.py:23
  46.7 13.6 %collective-permute-start.9 = (f32[40,4096]{1,0:T(8,128)S(1)}, f32[40,4096]{1,0:T(8,128)S(1)}, u32[]{:S(2)}, u32[]{:S(2)}) collective-permute-start(f32[40,4096]{1,0:T(8,128)S(1)} %maximum_dynamic-update-slice_fusion.3), channel_id=1, source_target_pairs={{0,8},{4,12},{8,16},{12,20},{16,24},{20,28},{24,0},{28,4},{32,40},... | collective-permute-start | bytes 1966088 | tf_op jit(solution)/shard_map/ppermute | solution.py:27
  48.0 16.6 %collective-permute-start.21 = (f32[32,4096]{1,0:T(8,128)S(1)}, f32[32,4096]{1,0:T(8,128)S(1)}, u32[]{:S(2)}, u32[]{:S(2)}) collective-permute-start(f32[32,4096]{1,0:T(8,128)S(1)} %maximum_maximum_fusion), channel_id=1, source_target_pairs={{0,224},{4,228},{8,232},{12,236},{16,240},{20,244},{24,248},{28,25... | collective-permute-start | bytes 1572872 | tf_op jit(solution)/shard_map/ppermute | solution.py:23
  51.0 13.9 %collective-permute-start.11 = (f32[40,4096]{1,0:T(8,128)S(1)}, f32[40,4096]{1,0:T(8,128)S(1)}, u32[]{:S(2)}, u32[]{:S(2)}) collective-permute-start(f32[40,4096]{1,0:T(8,128)S(1)} %maximum_dynamic-update-slice_fusion.3), channel_id=1, source_target_pairs={{0,24},{4,28},{8,0},{12,4},{16,8},{20,12},{24,16},{28,20},{32,56},... | collective-permute-start | bytes 1966088 | tf_op jit(solution)/shard_map/ppermute | solution.py:27
  60.2 8.1 %collective-permute-start.12 = (f32[24,2048]{1,0:T(8,128)S(1)}, f32[24,2048]{1,0:T(8,128)S(1)}, u32[]{:S(2)}, u32[]{:S(2)}) collective-permute-start(f32[24,2048]{1,0:T(8,128)S(1)} %slice.68), channel_id=1, source_target_pairs={{0,8},{4,12},{8,16},{12,20},{16,24},{20,28},{24,0},{28,4},{32,40},... | collective-permute-start | bytes 589832 | tf_op jit(solution)/shard_map/ppermute | solution.py:27
  61.9 7.5 %collective-permute-start.13 = (f32[24,2048]{1,0:T(8,128)S(1)}, f32[24,2048]{1,0:T(8,128)S(1)}, u32[]{:S(2)}, u32[]{:S(2)}) collective-permute-start(f32[24,2048]{1,0:T(8,128)S(1)} %slice.69), channel_id=1, source_target_pairs={{0,24},{4,28},{8,0},{12,4},{16,8},{20,12},{24,16},{28,20},{32,56},... | collective-permute-start | bytes 589832 | tf_op jit(solution)/shard_map/ppermute | solution.py:27
  64.6 9.2 %collective-permute-start.22 = (f32[32,4096]{1,0:T(8,128)S(1)}, f32[32,4096]{1,0:T(8,128)S(1)}, u32[]{:S(2)}, u32[]{:S(2)}) collective-permute-start(f32[32,4096]{1,0:T(8,128)S(1)} %collective-permute-done.20), channel_id=1, source_target_pairs={{0,32},{4,36},{8,40},{12,44},{16,48},{20,52},{24,56},{28,60},{32,6... | collective-permute-start | bytes 1572872 | tf_op jit(solution)/shard_map/ppermute | solution.py:23
  65.0 9.0 %collective-permute-start.23 = (f32[32,4096]{1,0:T(8,128)S(1)}, f32[32,4096]{1,0:T(8,128)S(1)}, u32[]{:S(2)}, u32[]{:S(2)}) collective-permute-start(f32[32,4096]{1,0:T(8,128)S(1)} %collective-permute-done.21), channel_id=1, source_target_pairs={{0,224},{4,228},{8,232},{12,236},{16,240},{20,244},{24,248},{28,25... | collective-permute-start | bytes 1572872 | tf_op jit(solution)/shard_map/ppermute | solution.py:23
  68.3 8.6 %collective-permute-start.14 = (f32[40,2048]{1,0:T(8,128)S(1)}, f32[40,2048]{1,0:T(8,128)S(1)}, u32[]{:S(2)}, u32[]{:S(2)}) collective-permute-start(f32[40,2048]{1,0:T(8,128)S(1)} %slice.70), channel_id=1, source_target_pairs={{0,8},{4,12},{8,16},{12,20},{16,24},{20,28},{24,0},{28,4},{32,40},... | collective-permute-start | bytes 983048 | tf_op jit(solution)/shard_map/ppermute | solution.py:27
  69.4 7.5 %collective-permute-start.15 = (f32[40,2048]{1,0:T(8,128)S(1)}, f32[40,2048]{1,0:T(8,128)S(1)}, u32[]{:S(2)}, u32[]{:S(2)}) collective-permute-start(f32[40,2048]{1,0:T(8,128)S(1)} %slice.71), channel_id=1, source_target_pairs={{0,24},{4,28},{8,0},{12,4},{16,8},{20,12},{24,16},{28,20},{32,56},... | collective-permute-start | bytes 983048 | tf_op jit(solution)/shard_map/ppermute | solution.py:27
  73.9 12.3 %collective-permute-start.24 = (f32[32,4096]{1,0:T(8,128)S(1)}, f32[32,4096]{1,0:T(8,128)S(1)}, u32[]{:S(2)}, u32[]{:S(2)}) collective-permute-start(f32[32,4096]{1,0:T(8,128)S(1)} %collective-permute-done.22), channel_id=1, source_target_pairs={{0,32},{4,36},{8,40},{12,44},{16,48},{20,52},{24,56},{28,60},{32,6... | collective-permute-start | bytes 1572872 | tf_op jit(solution)/shard_map/ppermute | solution.py:23
  73.9 12.4 %collective-permute-start.25 = (f32[32,4096]{1,0:T(8,128)S(1)}, f32[32,4096]{1,0:T(8,128)S(1)}, u32[]{:S(2)}, u32[]{:S(2)}) collective-permute-start(f32[32,4096]{1,0:T(8,128)S(1)} %collective-permute-done.23), channel_id=1, source_target_pairs={{0,224},{4,228},{8,232},{12,236},{16,240},{20,244},{24,248},{28,25... | collective-permute-start | bytes 1572872 | tf_op jit(solution)/shard_map/ppermute | solution.py:23
  86.2 9.7 %collective-permute-start.26 = (f32[32,2048]{1,0:T(8,128)S(1)}, f32[32,2048]{1,0:T(8,128)S(1)}, u32[]{:S(2)}, u32[]{:S(2)}) collective-permute-start(f32[32,2048]{1,0:T(8,128)S(1)} %slice.74), channel_id=1, source_target_pairs={{0,32},{4,36},{8,40},{12,44},{16,48},{20,52},{24,56},{28,60},{32,6... | collective-permute-start | bytes 786440 | tf_op jit(solution)/shard_map/ppermute | solution.py:23
  86.3 10.1 %collective-permute-start.27 = (f32[32,2048]{1,0:T(8,128)S(1)}, f32[32,2048]{1,0:T(8,128)S(1)}, u32[]{:S(2)}, u32[]{:S(2)}) collective-permute-start(f32[32,2048]{1,0:T(8,128)S(1)} %slice.75), channel_id=1, source_target_pairs={{0,224},{4,228},{8,232},{12,236},{16,240},{20,244},{24,248},{28,25... | collective-permute-start | bytes 786440 | tf_op jit(solution)/shard_map/ppermute | solution.py:23
  97.3 10.7 %copy-start.1 = (f32[512,4096]{1,0:T(8,128)S(1)}, f32[512,4096]{1,0:T(8,128)}, u32[]{:S(2)}) copy-start(f32[512,4096]{1,0:T(8,128)} %maximum_dynamic-update-slice_fusion.1) | copy-start | bytes 25165828
  118.5 6.5 %collective-permute-start.29 = (f32[512,128]{1,0:T(8,128)S(1)}, f32[512,128]{1,0:T(8,128)S(1)}, u32[]{:S(2)}, u32[]{:S(2)}) collective-permute-start(f32[512,128]{1,0:T(8,128)S(1)} %bitcast.81), channel_id=1, source_target_pairs={{0,1},{1,2},{2,3},{3,0},{4,5},{5,6},{6,7},{7,4},{8,9},{9,10},{10,1... | collective-permute-start | bytes 786440 | tf_op jit(solution)/shard_map/ppermute | solution.py:35
  119.9 5.3 %collective-permute-start.30 = (f32[512,128]{1,0:T(8,128)S(1)}, f32[512,128]{1,0:T(8,128)S(1)}, u32[]{:S(2)}, u32[]{:S(2)}) collective-permute-start(f32[512,128]{1,0:T(8,128)S(1)} %bitcast.82), channel_id=1, source_target_pairs={{0,3},{1,0},{2,1},{3,2},{4,7},{5,4},{6,5},{7,6},{8,11},{9,8},{10,9... | collective-permute-start | bytes 786440 | tf_op jit(solution)/shard_map/ppermute | solution.py:35
  121.6 7.2 %collective-permute-start.31 = (f32[512,128]{1,0:T(8,128)S(1)}, f32[512,128]{1,0:T(8,128)S(1)}, u32[]{:S(2)}, u32[]{:S(2)}) collective-permute-start(f32[512,128]{1,0:T(8,128)S(1)} %bitcast.83), channel_id=1, source_target_pairs={{0,2},{1,3},{2,0},{3,1},{4,6},{5,7},{6,4},{7,5},{8,10},{9,11},{10,... | collective-permute-start | bytes 786440 | tf_op jit(solution)/shard_map/ppermute | solution.py:35
  128.8 11.7 %collective-permute-start.32 = (f32[512,128]{1,0:T(8,128)S(1)}, f32[512,128]{1,0:T(8,128)S(1)}, u32[]{:S(2)}, u32[]{:S(2)}) collective-permute-start(f32[512,128]{1,0:T(8,128)S(1)} %fusion.5), channel_id=1, source_target_pairs={{0,4},{4,0},{8,12},{12,8},{16,20},{20,16},{24,28},{28,24},{32,36},... | collective-permute-start | bytes 786440 | tf_op jit(solution)/shard_map/ppermute | solution.py:31

commit v2 on v1

v2 whole, which is shorter than its diff:
```python
import jax
import jax.numpy as jnp
from jax import lax
from jax.sharding import PartitionSpec as P

NZ, NY, NC, NX = 8, 4, 2, 4
BR = 8
G = 64


def wide_pairs(dz, dy, swap=False):
    pairs = []
    for z in range(NZ):
        for y in range(NY):
            for c in range(NC):
                way = 1 if c == 0 else -1
                source = (z * NY + y) * NC + c
                chip = ((z + way * dz) % NZ) * NY + (y + way * dy) % NY
                pairs.append((source, chip * NC + (1 - c if swap else c)))
    return pairs


def along_z(block):
    return lax.ppermute(block, "wide", wide_pairs(1, 0))


def along_y(block):
    return lax.ppermute(block, "wide", wide_pairs(0, 1))


def other_core(block):
    return lax.ppermute(block, "wide", wide_pairs(0, 0, True))


def along_x(block, step):
    return lax.ppermute(block, "narrow", [(i, (i + step) % NX) for i in range(NX)])


def after(block, *earlier):
    return lax.optimization_barrier((block, *earlier))[0]


def halves(block):
    high = lax.reduce_precision(block, 8, 7)
    return high.astype(jnp.bfloat16), (block - high).astype(jnp.bfloat16)


def on_device(stored_amps, integrals, pair_counts, block_map):
    place = lax.axis_index("wide")
    layer = lax.axis_index("narrow")
    core = place % NC
    my_y = (place // NC) % NY
    my_z = place // (NC * NY)
    width = stored_amps.shape[1]

    sibling = other_core(stored_amps)
    theirs = other_core(after(integrals, sibling))
    top, low = stored_amps[:BR], stored_amps[BR:]

    def by_core(mine, others):
        return jnp.concatenate(
            [jnp.where(core == 0, mine, others), jnp.where(core == 0, others, mine)], axis=0
        )

    tops = by_core(top, sibling[:BR])
    lows = by_core(low, sibling[BR:])

    def mine_of(block):
        size = block.shape[0] // NC
        return lax.dynamic_slice_in_dim(block, core * size, size, 0)

    live = jnp.arange(width, dtype=jnp.int32)[:, None] < pair_counts[layer]
    held = jnp.where(live, jnp.concatenate([integrals, theirs], axis=1), jnp.float32(0.0))
    held_high, held_low = halves(held)

    def times(pieces):
        high, low_part = halves(jnp.concatenate(pieces, axis=0))
        count = high.shape[0]
        big = jnp.dot(
            jnp.concatenate([high, low_part], axis=0),
            held_high,
            preferred_element_type=jnp.float32,
        )
        small = jnp.dot(high, held_low, preferred_element_type=jnp.float32)
        return big[:count] + (big[count:] + small)

    t1 = along_z(tops)
    l1 = along_y(lows)
    t2 = along_z(t1)
    l2 = along_y(mine_of(l1))
    first = jnp.concatenate([top, t1], axis=0)
    f1 = along_y(after(first, l1))
    row_own = jnp.concatenate([low, l1, l2], axis=0)
    row_other = other_core(row_own)
    t3 = along_z(t2)
    a1 = along_z(after(row_own, t2))
    t4 = along_z(mine_of(t3))
    second = jnp.concatenate([t2, t3, t4], axis=0)
    b1 = along_z(after(row_other, t3))
    f2 = along_y(after(f1, t3))
    s1 = along_y(second)
    a2 = along_z(after(a1, held_high, held_low))
    f3 = along_y(f2)
    b2 = along_z(b1)
    s2 = along_y(s1)
    near = times([first, second, f1, s1, row_own, by_core(a1, b1)])
    a3 = along_z(a2)
    b3 = along_z(after(b2, near))
    s3 = along_y(after(s2, near))
    middle = times([f2, s2, by_core(a2, b2)])
    a4 = along_z(after(a3, middle))
    parts = [near, middle, times([f3, s3, by_core(a3, b3), a4])]
    cycle = jnp.concatenate(parts, axis=0)
    count = cycle.shape[0]
    span = NX * G
    chunks = jnp.stack(
        [
            jnp.concatenate(
                [cycle[:, a * G : (a + 1) * G], cycle[:, span + a * G : span + (a + 1) * G]], axis=1
            )
            for a in range(NX)
        ]
    )

    def chunk(step):
        return lax.dynamic_index_in_dim(chunks, (layer + step) % NX, 0, keepdims=False)

    total = chunk(0)
    for step in (1, 3, 2):
        total = total + along_x(chunk(step), step)
    total = jnp.where(core == 0, total, jnp.roll(total, G, axis=1))

    blocks = by_core(total, other_core(total)).reshape(NC * (count // BR), BR, 2 * G)

    target = jnp.arange(NZ * NY * NC, dtype=jnp.int32)
    pairs = target.shape[0] // 2
    owner = block_map[2 * (target % pairs) + core]
    their_core = owner % NC
    dz = (my_z - owner // (NC * NY)) % NZ
    dy = (my_y - (owner // NC) % NY) % NY
    is_top = target < pairs
    unit_low = jnp.array([0, 1, 3, 5], jnp.int32)[dy] + their_core * jnp.array(
        [4, 1, 4, 1], jnp.int32
    )[dy]
    side = jnp.where(is_top, their_core, unit_low // 4)
    holder = jnp.where(dz % 4 == 0, side, dz // 4)
    steps_z = jnp.where(holder == 0, dz, (NZ - dz) % NZ)
    steps_y = jnp.where(holder == 0, dy, (NY - dy) % NY)
    top_base = jnp.array([0, 8, 28, 44], jnp.int32)[steps_y]
    top_unit = jnp.where(
        steps_z == 0, 0, jnp.where(steps_z == 4, 7, 2 * steps_z - 1 + their_core)
    )
    low_base = jnp.array([16, 20, 36, 52, 60], jnp.int32)[steps_z]
    low_unit = jnp.where(steps_z % 4 == 0, unit_low % 4, unit_low)
    at = jnp.where(is_top, top_base + top_unit, low_base + low_unit) + holder * (count // BR)
    sent = jnp.take(blocks, at, axis=0, mode="clip")
    got = lax.all_to_all(sent, "wide", split_axis=0, concat_axis=0, tiled=True)
    got = got.reshape(NZ * NY, NC, BR, 2 * G)
    return jnp.transpose(got, (1, 2, 0, 3)).reshape(NC * BR, NZ * NY * 2 * G)


def solution(mesh):
    placed = (P("wide", "narrow"), P("narrow", "wide"), P(), P())
    return jax.shard_map(
        on_device, mesh=mesh, in_specs=placed, out_specs=P("wide", "narrow"), check_vma=False
    )
```

time: 164 us -> 137 us (0.84)
  waiting for transfers between devices: 30.3 us -> 48.6 us
  local copies, waits for them, and re-layouts: 22.7 us -> 5.99 us
  matrix products: 20.9 us -> 7.56 us
  starting transfers between devices: 60.5 us -> 48.3 us
  blocking collectives: 21.4 us -> 19.7 us
    ppermute x30 -> x23, waiting for transfers between devices: 25.6 us -> 44 us  [the longest x11 30.7 us: along_z(): return lax.ppermute(block, 'wide', wide_pairs(1, 0))]
    unnamed x30 -> x18, local copies, waits for them, and re-layouts: 17.7 us -> 2.67 us
    dot_general x2 -> x6, matrix products: 20.9 us -> 7.56 us  [the longest x3 4.84 us: times(): jnp.dot(jnp.concatenate([high, low_part], axis=0), held_high, preferred_e...]
    ppermute x30 -> x23, starting transfers between devices: 56.1 us -> 43.1 us  [the longest x11 23.3 us: along_z(): return lax.ppermute(block, 'wide', wide_pairs(1, 0))]
    select_n x1 -> x3, other arithmetic: 3.87 us -> 0.25 us  [the longest x1 0.14 us: on_device(): total = jnp.where(core == 0, total, jnp.roll(total, G, axis=1))]
    convert_element_type x0 -> x4, other arithmetic: none -> 2.97 us  [halves(): return (high.astype(jnp.bfloat16), (block - high).astype(jnp.bfloat16))]
  transfers between devices with their start and end apart: 33 -> 26, of which waited for: 15 -> 15; matrix products, arithmetic and copies ran while one was open for 23% -> 9% of each run, Pallas kernels for 0% -> 0%
where the time goes in v2:
time: 137 us
  waiting for transfers between devices  48.6 us (35%)
  starting transfers between devices  48.3 us (35%)
  blocking collectives  19.7 us (14%)
  matrix products  7.56 us (6%)
  local copies, waits for them, and re-layouts  5.99 us (4%)
  other arithmetic  5.99 us (4%)
    ppermute x11, waiting for transfers between devices, along_z(): return lax.ppermute(block, 'wide', wide_pairs(1, 0))  30.7 us
    ppermute x11, starting transfers between devices, along_z(): return lax.ppermute(block, 'wide', wide_pairs(1, 0))  23.3 us
    all_to_all x1, blocking collectives, on_device(): got = lax.all_to_all(sent, 'wide', split_axis=0, concat_axis=0, tiled=True)  19.7 us
    ppermute x4, starting transfers between devices, other_core(): return lax.ppermute(block, 'wide', wide_pairs(0, 0, True))  14.2 us
    ppermute x8, waiting for transfers between devices, along_y(): return lax.ppermute(block, 'wide', wide_pairs(0, 1))  12.2 us
    ppermute x8, starting transfers between devices, along_y(): return lax.ppermute(block, 'wide', wide_pairs(0, 1))  5.68 us
    ppermute x3, starting transfers between devices, along_x(): lax.ppermute(block, 'narrow', [(i, (i + step) % NX) for i in range(NX)])  5.12 us
    dot_general x3, matrix products, times(): jnp.dot(jnp.concatenate([high, low_part], axis=0), held_high, preferred_e...  4.84 us
  transfers between devices with their start and end apart: 26, of which 15 were waited for; matrix products, arithmetic and copies ran while one was open for 9% of the time, Pallas kernels for 0%

profile of v2, /device:TPU:1, one launch (start us, length us, event | category | flops | bytes accessed | tf_op | source)
XLA Modules:
  0.0 136.6 jit_solution(12827875564032816691)
XLA Ops:
  0.0 3.2 %collective-permute-start = (f32[16,4096]{1,0:T(8,128)}, f32[16,4096]{1,0:T(8,128)S(1)}, u32[]{:S(2)}, u32[]{:S(2)}) collective-permute-start(f32[16,4096]{1,0:T(8,128)} %param.8), channel_id=1, source_target_pairs={{0,4},{4,0},{8,12},{12,8},{16,20},{20,16},{24,28},{28,24},{32,36},... | collective-permute-start | bytes 786440 | tf_op jit(solution)/shard_map/ppermute | solution.py:32
  3.2 1.2 dynamic_slice.24
  4.5 0.7 iota_compare_fusion
  5.3 1.0 fusion.40
  6.3 1.1 collective-permute-start.5
  7.5 5.7 %collective-permute-start.1 = (f32[16,4096]{1,0:T(8,128)S(1)}, f32[16,4096]{1,0:T(8,128)S(1)}, u32[]{:S(2)}, u32[]{:S(2)}) collective-permute-start(f32[16,4096]{1,0:T(8,128)S(1)} %pad_maximum_fusion.6), channel_id=1, source_target_pairs={{0,32},{4,228},{8,40},{12,236},{16,48},{20,244},{24,56},{28,252},{... | collective-permute-start | bytes 786440 | tf_op jit(solution)/shard_map/ppermute | solution.py:24
  13.1 0.8 collective-permute-start.8
  14.0 2.5 %collective-permute-done.1 = f32[16,4096]{1,0:T(8,128)S(1)} collective-permute-done((f32[16,4096]{1,0:T(8,128)S(1)}, f32[16,4096]{1,0:T(8,128)S(1)}, u32[]{:S(2)}, u32[]{:S(2)}) %collective-permute-start.1) | collective-permute-done | bytes 262176 | tf_op jit(solution)/shard_map/ppermute | solution.py:24
  17.0 3.1 %collective-permute-start.2 = (f32[16,4096]{1,0:T(8,128)S(1)}, f32[16,4096]{1,0:T(8,128)S(1)}, u32[]{:S(2)}, u32[]{:S(2)}) collective-permute-start(f32[16,4096]{1,0:T(8,128)S(1)} %collective-permute-done.1), channel_id=1, source_target_pairs={{0,32},{4,228},{8,40},{12,236},{16,48},{20,244},{24,56},{28,252},{... | collective-permute-start | bytes 786440 | tf_op jit(solution)/shard_map/ppermute | solution.py:24
  20.2 0.7 collective-permute-start.10
  20.9 2.6 %collective-permute-done.2 = f32[16,4096]{1,0:T(8,128)S(1)} collective-permute-done((f32[16,4096]{1,0:T(8,128)S(1)}, f32[16,4096]{1,0:T(8,128)S(1)}, u32[]{:S(2)}, u32[]{:S(2)}) %collective-permute-start.2) | collective-permute-done | bytes 262176 | tf_op jit(solution)/shard_map/ppermute | solution.py:24
  23.5 3.4 %collective-permute-start.9 = (f32[32,4096]{1,0:T(8,128)S(1)}, f32[32,4096]{1,0:T(8,128)S(1)}, u32[]{:S(2)}, u32[]{:S(2)}) collective-permute-start(f32[32,4096]{1,0:T(8,128)S(1)} %pad_maximum_fusion.4), channel_id=1, source_target_pairs={{0,32},{4,228},{8,40},{12,236},{16,48},{20,244},{24,56},{28,252},{... | collective-permute-start | bytes 1572872 | tf_op jit(solution)/shard_map/ppermute | solution.py:24
  26.9 8.9 %collective-permute-done.3 = f32[16,4096]{1,0:T(8,128)S(1)} collective-permute-done((f32[16,4096]{1,0:T(8,128)S(1)}, f32[16,4096]{1,0:T(8,128)S(1)}, u32[]{:S(2)}, u32[]{:S(2)}) %collective-permute-start.3) | collective-permute-done | bytes 262176 | tf_op jit(solution)/shard_map/ppermute | solution.py:24
  35.8 3.2 %collective-permute-start.4 = (f32[8,4096]{1,0:T(8,128)S(1)}, f32[8,4096]{1,0:T(8,128)S(1)}, u32[]{:S(2)}, u32[]{:S(2)}) collective-permute-start(f32[8,4096]{1,0:T(8,128)S(1)} %constant_dynamic-slice_fusion.1), channel_id=1, source_target_pairs={{0,32},{4,228},{8,40},{12,236},{16,48},{20,244},{24,56},{28,252},{... | collective-permute-start | bytes 393224 | tf_op jit(solution)/shard_map/ppermute | solution.py:24
  39.2 1.7 %collective-permute-done.4 = f32[8,4096]{1,0:T(8,128)S(1)} collective-permute-done((f32[8,4096]{1,0:T(8,128)S(1)}, f32[8,4096]{1,0:T(8,128)S(1)}, u32[]{:S(2)}, u32[]{:S(2)}) %collective-permute-start.4) | collective-permute-done | bytes 131104 | tf_op jit(solution)/shard_map/ppermute | solution.py:24
  41.1 4.8 %collective-permute-done.13 = f32[24,4096]{1,0:T(8,128)S(1)} collective-permute-done((f32[24,4096]{1,0:T(8,128)S(1)}, f32[24,4096]{1,0:T(8,128)S(1)}, u32[]{:S(2)}, u32[]{:S(2)}) %collective-permute-start.13) | collective-permute-done | bytes 393248 | tf_op jit(solution)/shard_map/ppermute | solution.py:28
  45.9 0.9 collective-permute-start.17
  47.4 2.5 %collective-permute-start.16 = (f32[32,4096]{1,0:T(8,128)S(1)}, f32[32,4096]{1,0:T(8,128)S(1)}, u32[]{:S(2)}, u32[]{:S(2)}) collective-permute-start(f32[32,4096]{1,0:T(8,128)S(1)} %collective-permute-done.11), channel_id=1, source_target_pairs={{0,32},{4,228},{8,40},{12,236},{16,48},{20,244},{24,56},{28,252},{... | collective-permute-start | bytes 1572872 | tf_op jit(solution)/shard_map/ppermute | solution.py:24
  49.9 3.0 %collective-permute-done.7 = f32[40,4096]{1,0:T(8,128)S(1)} collective-permute-done((f32[40,4096]{1,0:T(8,128)S(1)}, f32[40,4096]{1,0:T(8,128)S(1)}, u32[]{:S(2)}, u32[]{:S(2)}) %collective-permute-start.7) | collective-permute-done | bytes 655392 | tf_op jit(solution)/shard_map/ppermute | solution.py:28
  53.0 1.2 collective-permute-start.14
  54.2 2.9 %collective-permute-done.17 = f32[24,4096]{1,0:T(8,128)S(1)} collective-permute-done((f32[24,4096]{1,0:T(8,128)S(1)}, f32[24,4096]{1,0:T(8,128)S(1)}, u32[]{:S(2)}, u32[]{:S(2)}) %collective-permute-start.17) | collective-permute-done | bytes 393248 | tf_op jit(solution)/shard_map/ppermute | solution.py:28
  58.0 1.6 %copy-done.1 = f32[4096,256]{1,0:T(8,128)S(1)} copy-done((f32[4096,256]{1,0:T(8,128)S(1)}, f32[4096,256]{1,0:T(8,128)}, u32[]{:S(2)}) %copy-start.1) | copy-done | bytes 4194328
  59.5 1.6 %reduce-precision_convert_fusion = (bf16[4096,512]{1,0:T(8,128)(2,1)S(1)}, bf16[4096,512]{1,0:T(8,128)(2,1)S(1)}) fusion(f32[4096,256]{1,0:T(8,128)S(1)} %collective-permute-done.12, f32[4096,256]{1,0:T(8,128)S(1)} %copy-done.1, pred[4096]{0:T(1024)(128)(4,1)S(1)} %iota_compare_fusion), kind=kLoop, calls=%fused_computation.3 | loop fusion | flops 12582912 | bytes 16781312 | tf_op jit(solution)/shard_map/convert_element_type | solution.py:45
  61.1 1.0 collective-permute-start.15
  62.1 2.0 %fusion.2 = f32[448,512]{1,0:T(8,128)S(1)} fusion(bf16[4096,512]{1,0:T(8,128)(2,1)S(1)} %get-tuple-element.23, bf16[224,4096]{1,0:T(8,128)(2,1)S(1)} %get-tuple-element.25, bf16[224,4096]{1,0:T(8,128)(2,1)S(1)} %get-tuple-element.26), kind=kOutput, calls=%fused_computation.11 | convolution fusion | flops 1886388224 | bytes 8781824 | tf_op jit(solution)/shard_map/dot_general | solution.py:79
  64.2 1.1 fusion.16
  65.4 1.0 collective-permute-start.18
  66.4 3.0 %collective-permute-done.15 = f32[32,4096]{1,0:T(8,128)S(1)} collective-permute-done((f32[32,4096]{1,0:T(8,128)S(1)}, f32[32,4096]{1,0:T(8,128)S(1)}, u32[]{:S(2)}, u32[]{:S(2)}) %collective-permute-start.15) | collective-permute-done | bytes 524320 | tf_op jit(solution)/shard_map/ppermute | solution.py:24
  69.4 1.9 %collective-permute-start.19 = (f32[32,4096]{1,0:T(8,128)S(1)}, f32[32,4096]{1,0:T(8,128)S(1)}, u32[]{:S(2)}, u32[]{:S(2)}) collective-permute-start(f32[32,4096]{1,0:T(8,128)S(1)} %collective-permute-done.15), channel_id=1, source_target_pairs={{0,32},{4,228},{8,40},{12,236},{16,48},{20,244},{24,56},{28,252},{... | collective-permute-start | bytes 1572872 | tf_op jit(solution)/shard_map/ppermute | solution.py:24
  71.8 1.2 fusion.12
  73.0 0.7 fusion.18
  73.8 1.5 %collective-permute-done.18 = f32[40,4096]{1,0:T(8,128)S(1)} collective-permute-done((f32[40,4096]{1,0:T(8,128)S(1)}, f32[40,4096]{1,0:T(8,128)S(1)}, u32[]{:S(2)}, u32[]{:S(2)}) %collective-permute-start.18) | collective-permute-done | bytes 655392 | tf_op jit(solution)/shard_map/ppermute | solution.py:28
  75.3 5.5 %collective-permute-done.19 = f32[32,4096]{1,0:T(8,128)S(1)} collective-permute-done((f32[32,4096]{1,0:T(8,128)S(1)}, f32[32,4096]{1,0:T(8,128)S(1)}, u32[]{:S(2)}, u32[]{:S(2)}) %collective-permute-start.19) | collective-permute-done | bytes 524320 | tf_op jit(solution)/shard_map/ppermute | solution.py:24
  80.8 2.1 %collective-permute-start.21 = (f32[32,4096]{1,0:T(8,128)S(1)}, f32[32,4096]{1,0:T(8,128)S(1)}, u32[]{:S(2)}, u32[]{:S(2)}) collective-permute-start(f32[32,4096]{1,0:T(8,128)S(1)} %collective-permute-done.19), channel_id=1, source_target_pairs={{0,32},{4,228},{8,40},{12,236},{16,48},{20,244},{24,56},{28,252},{... | collective-permute-start | bytes 1572872 | tf_op jit(solution)/shard_map/ppermute | solution.py:24
  83.0 6.0 %collective-permute-done.21 = f32[32,4096]{1,0:T(8,128)S(1)} collective-permute-done((f32[32,4096]{1,0:T(8,128)S(1)}, f32[32,4096]{1,0:T(8,128)S(1)}, u32[]{:S(2)}, u32[]{:S(2)}) %collective-permute-start.21) | collective-permute-done | bytes 524320 | tf_op jit(solution)/shard_map/ppermute | solution.py:24
  89.5 1.5 %fusion.7 = f32[320,512]{1,0:T(8,128)S(1)} fusion(bf16[4096,512]{1,0:T(8,128)(2,1)S(1)} %get-tuple-element.23, bf16[160,4096]{1,0:T(8,128)(2,1)S(1)} %get-tuple-element.27, bf16[160,4096]{1,0:T(8,128)(2,1)S(1)} %get-tuple-element.28), kind=kOutput, calls=%fused_computation.18 | convolution fusion | flops 1347420160 | bytes 7471104 | tf_op jit(solution)/shard_map/dot_general | solution.py:79
  91.1 0.9 fusion.17
  93.0 1.5 %collective-permute-start.22 = (f32[512,128]{1,0:T(8,128)S(1)}, f32[512,128]{1,0:T(8,128)S(1)}, u32[]{:S(2)}, u32[]{:S(2)}) collective-permute-start(f32[512,128]{1,0:T(8,128)S(1)} %get-tuple-element.31), channel_id=1, source_target_pairs={{0,1},{1,2},{2,3},{3,0},{4,5},{5,6},{6,7},{7,4},{8,9},{9,10},{10,1... | collective-permute-start | bytes 786440 | tf_op jit(solution)/shard_map/ppermute | solution.py:36
  94.5 2.5 %collective-permute-start.24 = (f32[512,128]{1,0:T(8,128)S(1)}, f32[512,128]{1,0:T(8,128)S(1)}, u32[]{:S(2)}, u32[]{:S(2)}) collective-permute-start(f32[512,128]{1,0:T(8,128)S(1)} %get-tuple-element.32), channel_id=1, source_target_pairs={{0,2},{1,3},{2,0},{3,1},{4,6},{5,7},{6,4},{7,5},{8,10},{9,11},{10,... | collective-permute-start | bytes 786440 | tf_op jit(solution)/shard_map/ppermute | solution.py:36
  96.9 1.2 collective-permute-start.23
  98.1 0.8 gather_fusion
  98.9 0.8 collective-permute-done.22
  99.7 3.8 %collective-permute-done.24 = f32[512,128]{1,0:T(8,128)S(1)} collective-permute-done((f32[512,128]{1,0:T(8,128)S(1)}, f32[512,128]{1,0:T(8,128)S(1)}, u32[]{:S(2)}, u32[]{:S(2)}) %collective-permute-start.24) | collective-permute-done | bytes 262176 | tf_op jit(solution)/shard_map/ppermute | solution.py:36
  103.8 10.2 %collective-permute-start.25 = (f32[512,128]{1,0:T(8,128)S(1)}, f32[512,128]{1,0:T(8,128)S(1)}, u32[]{:S(2)}, u32[]{:S(2)}) collective-permute-start(f32[512,128]{1,0:T(8,128)S(1)} %maximum_select_fusion.1), channel_id=1, source_target_pairs={{0,4},{4,0},{8,12},{12,8},{16,20},{20,16},{24,28},{28,24},{32,36},... | collective-permute-start | bytes 786440 | tf_op jit(solution)/shard_map/ppermute | solution.py:32
  114.1 1.1 collective-permute-done.25
  115.2 0.6 gather_fusion.1
  115.9 19.7 %all_to_all.5 = f32[64,8,128]{2,1,0:T(8,128)S(1)} all-to-all(f32[64,8,128]{2,1,0:T(8,128)S(1)} %gather_fusion.1), channel_id=1, replica_groups=mesh['wide'=64,'narrow'=4] {'wide'}, dimensions={0} | all-to-all | bytes 524288 | tf_op jit(solution)/shard_map/all_to_all | solution.py:157
  135.7 0.9 copy.13
  (67 shorter events, 5.3 us)
Async XLA Ops:
  0.0 98.1 %copy-start = (s32[64]{0:T(128)S(1)}, s32[64]{0:T(128)}, u32[]{:S(2)}) copy-start(s32[64]{0:T(128)} %param.11) | copy-start | bytes 772
  0.0 5.1 %collective-permute-start = (f32[16,4096]{1,0:T(8,128)}, f32[16,4096]{1,0:T(8,128)S(1)}, u32[]{:S(2)}, u32[]{:S(2)}) collective-permute-start(f32[16,4096]{1,0:T(8,128)} %param.8), channel_id=1, source_target_pairs={{0,4},{4,0},{8,12},{12,8},{16,20},{20,16},{24,28},{28,24},{32,36},... | collective-permute-start | bytes 786440 | tf_op jit(solution)/shard_map/ppermute | solution.py:32
  5.1 52.8 %collective-permute-start.12 = (f32[4096,256]{1,0:T(8,128)}, f32[4096,256]{1,0:T(8,128)S(1)}, u32[]{:S(2)}, u32[]{:S(2)}) collective-permute-start(f32[4096,256]{1,0:T(8,128)} %param.9), channel_id=1, source_target_pairs={{0,4},{4,0},{8,12},{12,8},{16,20},{20,16},{24,28},{28,24},{32,36},... | collective-permute-start | bytes 12582920 | tf_op jit(solution)/shard_map/ppermute | solution.py:32
  6.3 6.8 %collective-permute-start.5 = (f32[16,4096]{1,0:T(8,128)S(1)}, f32[16,4096]{1,0:T(8,128)S(1)}, u32[]{:S(2)}, u32[]{:S(2)}) collective-permute-start(f32[16,4096]{1,0:T(8,128)S(1)} %pad_maximum_fusion.7), channel_id=1, source_target_pairs={{0,8},{4,28},{8,16},{12,4},{16,24},{20,12},{24,0},{28,20},{32,40},... | collective-permute-start | bytes 786440 | tf_op jit(solution)/shard_map/ppermute | solution.py:28
  7.5 9.0 %collective-permute-start.1 = (f32[16,4096]{1,0:T(8,128)S(1)}, f32[16,4096]{1,0:T(8,128)S(1)}, u32[]{:S(2)}, u32[]{:S(2)}) collective-permute-start(f32[16,4096]{1,0:T(8,128)S(1)} %pad_maximum_fusion.6), channel_id=1, source_target_pairs={{0,32},{4,228},{8,40},{12,236},{16,48},{20,244},{24,56},{28,252},{... | collective-permute-start | bytes 786440 | tf_op jit(solution)/shard_map/ppermute | solution.py:24
  13.1 7.0 %collective-permute-start.8 = (f32[8,4096]{1,0:T(8,128)S(1)}, f32[8,4096]{1,0:T(8,128)S(1)}, u32[]{:S(2)}, u32[]{:S(2)}) collective-permute-start(f32[8,4096]{1,0:T(8,128)S(1)} %constant_dynamic-slice_fusion), channel_id=1, source_target_pairs={{0,8},{4,28},{8,16},{12,4},{16,24},{20,12},{24,0},{28,20},{32,40},... | collective-permute-start | bytes 393224 | tf_op jit(solution)/shard_map/ppermute | solution.py:28
  16.4 36.6 %copy-start.2 = (f32[16,4096]{1,0:T(8,128)S(1)}, f32[16,4096]{1,0:T(8,128)}, u32[]{:S(2)}) copy-start(f32[16,4096]{1,0:T(8,128)} %param.8) | copy-start | bytes 786436
  16.5 22.5 %collective-permute-start.6 = (f32[24,4096]{1,0:T(8,128)S(1)}, f32[24,4096]{1,0:T(8,128)S(1)}, u32[]{:S(2)}, u32[]{:S(2)}) collective-permute-start(f32[24,4096]{1,0:T(8,128)S(1)} %pad_maximum_fusion.5), channel_id=1, source_target_pairs={{0,8},{4,28},{8,16},{12,4},{16,24},{20,12},{24,0},{28,20},{32,40},... | collective-permute-start | bytes 1179656 | tf_op jit(solution)/shard_map/ppermute | solution.py:28
  17.0 6.4 %collective-permute-start.2 = (f32[16,4096]{1,0:T(8,128)S(1)}, f32[16,4096]{1,0:T(8,128)S(1)}, u32[]{:S(2)}, u32[]{:S(2)}) collective-permute-start(f32[16,4096]{1,0:T(8,128)S(1)} %collective-permute-done.1), channel_id=1, source_target_pairs={{0,32},{4,228},{8,40},{12,236},{16,48},{20,244},{24,56},{28,252},{... | collective-permute-start | bytes 786440 | tf_op jit(solution)/shard_map/ppermute | solution.py:24
  20.2 18.8 %collective-permute-start.10 = (f32[32,4096]{1,0:T(8,128)S(1)}, f32[32,4096]{1,0:T(8,128)S(1)}, u32[]{:S(2)}, u32[]{:S(2)}) collective-permute-start(f32[32,4096]{1,0:T(8,128)S(1)} %pad_maximum_fusion.4), channel_id=1, source_target_pairs={{0,4},{4,0},{8,12},{12,8},{16,20},{20,16},{24,28},{28,24},{32,36},... | collective-permute-start | bytes 1572872 | tf_op jit(solution)/shard_map/ppermute | solution.py:32
  23.5 33.7 %collective-permute-start.9 = (f32[32,4096]{1,0:T(8,128)S(1)}, f32[32,4096]{1,0:T(8,128)S(1)}, u32[]{:S(2)}, u32[]{:S(2)}) collective-permute-start(f32[32,4096]{1,0:T(8,128)S(1)} %pad_maximum_fusion.4), channel_id=1, source_target_pairs={{0,32},{4,228},{8,40},{12,236},{16,48},{20,244},{24,56},{28,252},{... | collective-permute-start | bytes 1572872 | tf_op jit(solution)/shard_map/ppermute | solution.py:24
  26.9 8.9 %collective-permute-start.3 = (f32[16,4096]{1,0:T(8,128)S(1)}, f32[16,4096]{1,0:T(8,128)S(1)}, u32[]{:S(2)}, u32[]{:S(2)}) collective-permute-start(f32[16,4096]{1,0:T(8,128)S(1)} %collective-permute-done.2), channel_id=1, source_target_pairs={{0,32},{4,228},{8,40},{12,236},{16,48},{20,244},{24,56},{28,252},{... | collective-permute-start | bytes 786440 | tf_op jit(solution)/shard_map/ppermute | solution.py:24
  35.8 5.1 %collective-permute-start.4 = (f32[8,4096]{1,0:T(8,128)S(1)}, f32[8,4096]{1,0:T(8,128)S(1)}, u32[]{:S(2)}, u32[]{:S(2)}) collective-permute-start(f32[8,4096]{1,0:T(8,128)S(1)} %constant_dynamic-slice_fusion.1), channel_id=1, source_target_pairs={{0,32},{4,228},{8,40},{12,236},{16,48},{20,244},{24,56},{28,252},{... | collective-permute-start | bytes 393224 | tf_op jit(solution)/shard_map/ppermute | solution.py:24
  39.0 6.9 %collective-permute-start.13 = (f32[24,4096]{1,0:T(8,128)S(1)}, f32[24,4096]{1,0:T(8,128)S(1)}, u32[]{:S(2)}, u32[]{:S(2)}) collective-permute-start(f32[24,4096]{1,0:T(8,128)S(1)} %collective-permute-done.6), channel_id=1, source_target_pairs={{0,8},{4,28},{8,16},{12,4},{16,24},{20,12},{24,0},{28,20},{32,40},... | collective-permute-start | bytes 1179656 | tf_op jit(solution)/shard_map/ppermute | solution.py:28
  39.0 8.4 %collective-permute-start.11 = (f32[32,4096]{1,0:T(8,128)S(1)}, f32[32,4096]{1,0:T(8,128)S(1)}, u32[]{:S(2)}, u32[]{:S(2)}) collective-permute-start(f32[32,4096]{1,0:T(8,128)S(1)} %collective-permute-done.10), channel_id=1, source_target_pairs={{0,32},{4,228},{8,40},{12,236},{16,48},{20,244},{24,56},{28,252},{... | collective-permute-start | bytes 1572872 | tf_op jit(solution)/shard_map/ppermute | solution.py:24
  41.0 12.0 %collective-permute-start.7 = (f32[40,4096]{1,0:T(8,128)S(1)}, f32[40,4096]{1,0:T(8,128)S(1)}, u32[]{:S(2)}, u32[]{:S(2)}) collective-permute-start(f32[40,4096]{1,0:T(8,128)S(1)} %pad_maximum_fusion.3), channel_id=1, source_target_pairs={{0,8},{4,28},{8,16},{12,4},{16,24},{20,12},{24,0},{28,20},{32,40},... | collective-permute-start | bytes 1966088 | tf_op jit(solution)/shard_map/ppermute | solution.py:28
  45.9 11.2 %collective-permute-start.17 = (f32[24,4096]{1,0:T(8,128)S(1)}, f32[24,4096]{1,0:T(8,128)S(1)}, u32[]{:S(2)}, u32[]{:S(2)}) collective-permute-start(f32[24,4096]{1,0:T(8,128)S(1)} %collective-permute-done.13), channel_id=1, source_target_pairs={{0,8},{4,28},{8,16},{12,4},{16,24},{20,12},{24,0},{28,20},{32,40},... | collective-permute-start | bytes 1179656 | tf_op jit(solution)/shard_map/ppermute | solution.py:28
  47.4 17.9 %collective-permute-start.16 = (f32[32,4096]{1,0:T(8,128)S(1)}, f32[32,4096]{1,0:T(8,128)S(1)}, u32[]{:S(2)}, u32[]{:S(2)}) collective-permute-start(f32[32,4096]{1,0:T(8,128)S(1)} %collective-permute-done.11), channel_id=1, source_target_pairs={{0,32},{4,228},{8,40},{12,236},{16,48},{20,244},{24,56},{28,252},{... | collective-permute-start | bytes 1572872 | tf_op jit(solution)/shard_map/ppermute | solution.py:24
  53.0 12.4 %collective-permute-start.14 = (f32[40,4096]{1,0:T(8,128)S(1)}, f32[40,4096]{1,0:T(8,128)S(1)}, u32[]{:S(2)}, u32[]{:S(2)}) collective-permute-start(f32[40,4096]{1,0:T(8,128)S(1)} %collective-permute-done.7), channel_id=1, source_target_pairs={{0,8},{4,28},{8,16},{12,4},{16,24},{20,12},{24,0},{28,20},{32,40},... | collective-permute-start | bytes 1966088 | tf_op jit(solution)/shard_map/ppermute | solution.py:28
  57.3 2.2 %copy-start.1 = (f32[4096,256]{1,0:T(8,128)S(1)}, f32[4096,256]{1,0:T(8,128)}, u32[]{:S(2)}) copy-start(f32[4096,256]{1,0:T(8,128)} %param.9) | copy-start | bytes 12582916
  61.1 8.3 %collective-permute-start.15 = (f32[32,4096]{1,0:T(8,128)S(1)}, f32[32,4096]{1,0:T(8,128)S(1)}, u32[]{:S(2)}, u32[]{:S(2)}) collective-permute-start(f32[32,4096]{1,0:T(8,128)S(1)} %collective-permute-done.9), channel_id=1, source_target_pairs={{0,32},{4,228},{8,40},{12,236},{16,48},{20,244},{24,56},{28,252},{... | collective-permute-start | bytes 1572872 | tf_op jit(solution)/shard_map/ppermute | solution.py:24
  65.3 17.6 %collective-permute-start.20 = (f32[32,4096]{1,0:T(8,128)S(1)}, f32[32,4096]{1,0:T(8,128)S(1)}, u32[]{:S(2)}, u32[]{:S(2)}) collective-permute-start(f32[32,4096]{1,0:T(8,128)S(1)} %collective-permute-done.16), channel_id=1, source_target_pairs={{0,32},{4,228},{8,40},{12,236},{16,48},{20,244},{24,56},{28,252},{... | collective-permute-start | bytes 1572872 | tf_op jit(solution)/shard_map/ppermute | solution.py:24
  65.4 9.8 %collective-permute-start.18 = (f32[40,4096]{1,0:T(8,128)S(1)}, f32[40,4096]{1,0:T(8,128)S(1)}, u32[]{:S(2)}, u32[]{:S(2)}) collective-permute-start(f32[40,4096]{1,0:T(8,128)S(1)} %collective-permute-done.14), channel_id=1, source_target_pairs={{0,8},{4,28},{8,16},{12,4},{16,24},{20,12},{24,0},{28,20},{32,40},... | collective-permute-start | bytes 1966088 | tf_op jit(solution)/shard_map/ppermute | solution.py:28
  69.4 11.3 %collective-permute-start.19 = (f32[32,4096]{1,0:T(8,128)S(1)}, f32[32,4096]{1,0:T(8,128)S(1)}, u32[]{:S(2)}, u32[]{:S(2)}) collective-permute-start(f32[32,4096]{1,0:T(8,128)S(1)} %collective-permute-done.15), channel_id=1, source_target_pairs={{0,32},{4,228},{8,40},{12,236},{16,48},{20,244},{24,56},{28,252},{... | collective-permute-start | bytes 1572872 | tf_op jit(solution)/shard_map/ppermute | solution.py:24
  80.8 8.3 %collective-permute-start.21 = (f32[32,4096]{1,0:T(8,128)S(1)}, f32[32,4096]{1,0:T(8,128)S(1)}, u32[]{:S(2)}, u32[]{:S(2)}) collective-permute-start(f32[32,4096]{1,0:T(8,128)S(1)} %collective-permute-done.19), channel_id=1, source_target_pairs={{0,32},{4,228},{8,40},{12,236},{16,48},{20,244},{24,56},{28,252},{... | collective-permute-start | bytes 1572872 | tf_op jit(solution)/shard_map/ppermute | solution.py:24
  93.0 6.7 %collective-permute-start.22 = (f32[512,128]{1,0:T(8,128)S(1)}, f32[512,128]{1,0:T(8,128)S(1)}, u32[]{:S(2)}, u32[]{:S(2)}) collective-permute-start(f32[512,128]{1,0:T(8,128)S(1)} %get-tuple-element.31), channel_id=1, source_target_pairs={{0,1},{1,2},{2,3},{3,0},{4,5},{5,6},{6,7},{7,4},{8,9},{9,10},{10,1... | collective-permute-start | bytes 786440 | tf_op jit(solution)/shard_map/ppermute | solution.py:36
  94.5 9.0 %collective-permute-start.24 = (f32[512,128]{1,0:T(8,128)S(1)}, f32[512,128]{1,0:T(8,128)S(1)}, u32[]{:S(2)}, u32[]{:S(2)}) collective-permute-start(f32[512,128]{1,0:T(8,128)S(1)} %get-tuple-element.32), channel_id=1, source_target_pairs={{0,2},{1,3},{2,0},{3,1},{4,6},{5,7},{6,4},{7,5},{8,10},{9,11},{10,... | collective-permute-start | bytes 786440 | tf_op jit(solution)/shard_map/ppermute | solution.py:36
  96.9 6.6 %collective-permute-start.23 = (f32[512,128]{1,0:T(8,128)S(1)}, f32[512,128]{1,0:T(8,128)S(1)}, u32[]{:S(2)}, u32[]{:S(2)}) collective-permute-start(f32[512,128]{1,0:T(8,128)S(1)} %get-tuple-element.33), channel_id=1, source_target_pairs={{0,3},{1,0},{2,1},{3,2},{4,7},{5,4},{6,5},{7,6},{8,11},{9,8},{10,9... | collective-permute-start | bytes 786440 | tf_op jit(solution)/shard_map/ppermute | solution.py:36
  103.8 11.3 %collective-permute-start.25 = (f32[512,128]{1,0:T(8,128)S(1)}, f32[512,128]{1,0:T(8,128)S(1)}, u32[]{:S(2)}, u32[]{:S(2)}) collective-permute-start(f32[512,128]{1,0:T(8,128)S(1)} %maximum_select_fusion.1), channel_id=1, source_target_pairs={{0,4},{4,0},{8,12},{12,8},{16,20},{20,16},{24,28},{28,24},{32,36},... | collective-permute-start | bytes 786440 | tf_op jit(solution)/shard_map/ppermute | solution.py:32

commit v3 on v2

--- a/solution.py
+++ b/solution.py
@@ -99,35 +99,41 @@
     b1 = along_z(after(row_other, t3))
     f2 = along_y(after(f1, t3))
     s1 = along_y(second)
-    a2 = along_z(after(a1, held_high, held_low))
+    a2 = along_z(a1)
     f3 = along_y(f2)
     b2 = along_z(b1)
     s2 = along_y(s1)
     near = times([first, second, f1, s1, row_own, by_core(a1, b1)])
     a3 = along_z(a2)
-    b3 = along_z(after(b2, near))
+    b3 = along_z(b2)
     s3 = along_y(after(s2, near))
     middle = times([f2, s2, by_core(a2, b2)])
     a4 = along_z(after(a3, middle))
-    parts = [near, middle, times([f3, s3, by_core(a3, b3), a4])]
-    cycle = jnp.concatenate(parts, axis=0)
-    count = cycle.shape[0]
     span = NX * G
-    chunks = jnp.stack(
-        [
-            jnp.concatenate(
-                [cycle[:, a * G : (a + 1) * G], cycle[:, span + a * G : span + (a + 1) * G]], axis=1
-            )
-            for a in range(NX)
-        ]
-    )
 
-    def chunk(step):
-        return lax.dynamic_index_in_dim(chunks, (layer + step) % NX, 0, keepdims=False)
+    def layer_sum(cycle):
+        chunks = jnp.stack(
+            [
+                jnp.concatenate(
+                    [cycle[:, a * G : (a + 1) * G], cycle[:, span + a * G : span + (a + 1) * G]],
+                    axis=1,
+                )
+                for a in range(NX)
+            ]
+        )
 
-    total = chunk(0)
-    for step in (1, 3, 2):
-        total = total + along_x(chunk(step), step)
+        def chunk(step):
+            return lax.dynamic_index_in_dim(chunks, (layer + step) % NX, 0, keepdims=False)
+
+        total = chunk(0)
+        for step in (1, 3, 2):
+            total = total + along_x(chunk(step), step)
+        return total
+
+    early = layer_sum(jnp.concatenate([near, middle], axis=0))
+    late = layer_sum(times([f3, s3, by_core(a3, b3), a4]))
+    total = jnp.concatenate([early, late], axis=0)
+    count = total.shape[0]
     total = jnp.where(core == 0, total, jnp.roll(total, G, axis=1))
 
     blocks = by_core(total, other_core(total)).reshape(NC * (count // BR), BR, 2 * G)

time: 137 us -> 127 us (0.927)
  waiting for transfers between devices: 48.6 us -> 31.8 us
  starting transfers between devices: 48.3 us -> 55 us
  local copies, waits for them, and re-layouts: 5.99 us -> 4.14 us
  blocking collectives: 19.7 us -> 21.4 us
    ppermute x11, waiting for transfers between devices: 30.7 us -> 17.7 us  [along_z(): return lax.ppermute(block, 'wide', wide_pairs(1, 0))]
    ppermute x3 -> x6, starting transfers between devices: 5.12 us -> 11.1 us  [along_x(): lax.ppermute(block, 'narrow', [(i, (i + step) % NX) for i in range(NX)])]
    ppermute x8, waiting for transfers between devices: 12.2 us -> 9.74 us  [along_y(): return lax.ppermute(block, 'wide', wide_pairs(0, 1))]
    ppermute x4, starting transfers between devices: 14.2 us -> 12.1 us  [other_core(): return lax.ppermute(block, 'wide', wide_pairs(0, 0, True))]
    all_to_all x1, blocking collectives: 19.7 us -> 21.4 us  [on_device(): got = lax.all_to_all(sent, 'wide', split_axis=0, concat_axis=0, tiled=True)]
    unnamed x18, local copies, waits for them, and re-layouts: 2.67 us -> 1.13 us
    ppermute x11, starting transfers between devices: 23.3 us -> 24.8 us  [along_z(): return lax.ppermute(block, 'wide', wide_pairs(1, 0))]
    ppermute x3 -> x6, waiting for transfers between devices: 4.61 us -> 3.24 us  [along_x(): lax.ppermute(block, 'narrow', [(i, (i + step) % NX) for i in range(NX)])]
  transfers between devices with their start and end apart: 26 -> 29, of which waited for: 15 -> 15; matrix products, arithmetic and copies ran while one was open for 9% -> 13% of each run, Pallas kernels for 0% -> 0%
where the time goes in v3:
time: 127 us
  starting transfers between devices  55 us (43%)
  waiting for transfers between devices  31.8 us (25%)
  blocking collectives  21.4 us (17%)
  matrix products  7.55 us (6%)
  other arithmetic  6.41 us (5%)
  local copies, waits for them, and re-layouts  4.14 us (3%)
    ppermute x11, starting transfers between devices, along_z(): return lax.ppermute(block, 'wide', wide_pairs(1, 0))  24.8 us
    all_to_all x1, blocking collectives, on_device(): got = lax.all_to_all(sent, 'wide', split_axis=0, concat_axis=0, tiled=True)  21.4 us
    ppermute x11, waiting for transfers between devices, along_z(): return lax.ppermute(block, 'wide', wide_pairs(1, 0))  17.7 us
    ppermute x4, starting transfers between devices, other_core(): return lax.ppermute(block, 'wide', wide_pairs(0, 0, True))  12.1 us
    ppermute x6, starting transfers between devices, along_x(): lax.ppermute(block, 'narrow', [(i, (i + step) % NX) for i in range(NX)])  11.1 us
    ppermute x8, waiting for transfers between devices, along_y(): return lax.ppermute(block, 'wide', wide_pairs(0, 1))  9.74 us
    ppermute x8, starting transfers between devices, along_y(): return lax.ppermute(block, 'wide', wide_pairs(0, 1))  7.03 us
    dot_general x3, matrix products, times(): jnp.dot(jnp.concatenate([high, low_part], axis=0), held_high, preferred_e...  4.83 us
  transfers between devices with their start and end apart: 29, of which 15 were waited for; matrix products, arithmetic and copies ran while one was open for 13% of the time, Pallas kernels for 0%

profile of v3, /device:TPU:1, one launch (start us, length us, event | category | flops | bytes accessed | tf_op | source)
XLA Modules:
  0.0 126.7 jit_solution(14920047093555774788)
XLA Ops:
  0.0 3.2 %collective-permute-start = (f32[16,4096]{1,0:T(8,128)}, f32[16,4096]{1,0:T(8,128)S(1)}, u32[]{:S(2)}, u32[]{:S(2)}) collective-permute-start(f32[16,4096]{1,0:T(8,128)} %param.8), channel_id=1, source_target_pairs={{0,4},{4,0},{8,12},{12,8},{16,20},{20,16},{24,28},{28,24},{32,36},... | collective-permute-start | bytes 786440 | tf_op jit(solution)/shard_map/ppermute | solution.py:32
  3.3 1.2 dynamic_slice.37
  4.5 0.8 gather_fusion
  5.3 0.7 iota_compare_fusion.1
  6.2 1.0 fusion.53
  7.2 1.1 collective-permute-start.5
  8.3 5.7 %collective-permute-start.1 = (f32[16,4096]{1,0:T(8,128)S(1)}, f32[16,4096]{1,0:T(8,128)S(1)}, u32[]{:S(2)}, u32[]{:S(2)}) collective-permute-start(f32[16,4096]{1,0:T(8,128)S(1)} %pad_maximum_fusion.7), channel_id=1, source_target_pairs={{0,32},{4,228},{8,40},{12,236},{16,48},{20,244},{24,56},{28,252},{... | collective-permute-start | bytes 786440 | tf_op jit(solution)/shard_map/ppermute | solution.py:24
  14.0 0.8 collective-permute-start.8
  14.8 2.5 %collective-permute-done.1 = f32[16,4096]{1,0:T(8,128)S(1)} collective-permute-done((f32[16,4096]{1,0:T(8,128)S(1)}, f32[16,4096]{1,0:T(8,128)S(1)}, u32[]{:S(2)}, u32[]{:S(2)}) %collective-permute-start.1) | collective-permute-done | bytes 262176 | tf_op jit(solution)/shard_map/ppermute | solution.py:24
  17.9 3.1 %collective-permute-start.2 = (f32[16,4096]{1,0:T(8,128)S(1)}, f32[16,4096]{1,0:T(8,128)S(1)}, u32[]{:S(2)}, u32[]{:S(2)}) collective-permute-start(f32[16,4096]{1,0:T(8,128)S(1)} %collective-permute-done.1), channel_id=1, source_target_pairs={{0,32},{4,228},{8,40},{12,236},{16,48},{20,244},{24,56},{28,252},{... | collective-permute-start | bytes 786440 | tf_op jit(solution)/shard_map/ppermute | solution.py:24
  21.7 2.6 %collective-permute-done.2 = f32[16,4096]{1,0:T(8,128)S(1)} collective-permute-done((f32[16,4096]{1,0:T(8,128)S(1)}, f32[16,4096]{1,0:T(8,128)S(1)}, u32[]{:S(2)}, u32[]{:S(2)}) %collective-permute-start.2) | collective-permute-done | bytes 262176 | tf_op jit(solution)/shard_map/ppermute | solution.py:24
  24.3 3.4 %collective-permute-start.9 = (f32[32,4096]{1,0:T(8,128)S(1)}, f32[32,4096]{1,0:T(8,128)S(1)}, u32[]{:S(2)}, u32[]{:S(2)}) collective-permute-start(f32[32,4096]{1,0:T(8,128)S(1)} %pad_maximum_fusion.3), channel_id=1, source_target_pairs={{0,32},{4,228},{8,40},{12,236},{16,48},{20,244},{24,56},{28,252},{... | collective-permute-start | bytes 1572872 | tf_op jit(solution)/shard_map/ppermute | solution.py:24
  27.8 8.9 %collective-permute-done.3 = f32[16,4096]{1,0:T(8,128)S(1)} collective-permute-done((f32[16,4096]{1,0:T(8,128)S(1)}, f32[16,4096]{1,0:T(8,128)S(1)}, u32[]{:S(2)}, u32[]{:S(2)}) %collective-permute-start.3) | collective-permute-done | bytes 262176 | tf_op jit(solution)/shard_map/ppermute | solution.py:24
  36.7 3.2 %collective-permute-start.4 = (f32[8,4096]{1,0:T(8,128)S(1)}, f32[8,4096]{1,0:T(8,128)S(1)}, u32[]{:S(2)}, u32[]{:S(2)}) collective-permute-start(f32[8,4096]{1,0:T(8,128)S(1)} %constant_dynamic-slice_fusion.1), channel_id=1, source_target_pairs={{0,32},{4,228},{8,40},{12,236},{16,48},{20,244},{24,56},{28,252},{... | collective-permute-start | bytes 393224 | tf_op jit(solution)/shard_map/ppermute | solution.py:24
  40.1 1.7 %collective-permute-done.4 = f32[8,4096]{1,0:T(8,128)S(1)} collective-permute-done((f32[8,4096]{1,0:T(8,128)S(1)}, f32[8,4096]{1,0:T(8,128)S(1)}, u32[]{:S(2)}, u32[]{:S(2)}) %collective-permute-start.4) | collective-permute-done | bytes 131104 | tf_op jit(solution)/shard_map/ppermute | solution.py:24
  42.0 3.2 %collective-permute-start.15 = (f32[32,4096]{1,0:T(8,128)S(1)}, f32[32,4096]{1,0:T(8,128)S(1)}, u32[]{:S(2)}, u32[]{:S(2)}) collective-permute-start(f32[32,4096]{1,0:T(8,128)S(1)} %collective-permute-done.9), channel_id=1, source_target_pairs={{0,32},{4,228},{8,40},{12,236},{16,48},{20,244},{24,56},{28,252},{... | collective-permute-start | bytes 1572872 | tf_op jit(solution)/shard_map/ppermute | solution.py:24
  45.2 1.6 %collective-permute-done.13 = f32[24,4096]{1,0:T(8,128)S(1)} collective-permute-done((f32[24,4096]{1,0:T(8,128)S(1)}, f32[24,4096]{1,0:T(8,128)S(1)}, u32[]{:S(2)}, u32[]{:S(2)}) %collective-permute-start.13) | collective-permute-done | bytes 393248 | tf_op jit(solution)/shard_map/ppermute | solution.py:28
  46.8 1.2 collective-permute-start.20
  48.3 2.5 %collective-permute-start.16 = (f32[32,4096]{1,0:T(8,128)S(1)}, f32[32,4096]{1,0:T(8,128)S(1)}, u32[]{:S(2)}, u32[]{:S(2)}) collective-permute-start(f32[32,4096]{1,0:T(8,128)S(1)} %collective-permute-done.11), channel_id=1, source_target_pairs={{0,32},{4,228},{8,40},{12,236},{16,48},{20,244},{24,56},{28,252},{... | collective-permute-start | bytes 1572872 | tf_op jit(solution)/shard_map/ppermute | solution.py:24
  50.8 3.0 %collective-permute-done.7 = f32[40,4096]{1,0:T(8,128)S(1)} collective-permute-done((f32[40,4096]{1,0:T(8,128)S(1)}, f32[40,4096]{1,0:T(8,128)S(1)}, u32[]{:S(2)}, u32[]{:S(2)}) %collective-permute-start.7) | collective-permute-done | bytes 655392 | tf_op jit(solution)/shard_map/ppermute | solution.py:28
  54.7 1.3 %collective-permute-start.14 = (f32[40,4096]{1,0:T(8,128)S(1)}, f32[40,4096]{1,0:T(8,128)S(1)}, u32[]{:S(2)}, u32[]{:S(2)}) collective-permute-start(f32[40,4096]{1,0:T(8,128)S(1)} %collective-permute-done.7), channel_id=1, source_target_pairs={{0,8},{4,28},{8,16},{12,4},{16,24},{20,12},{24,0},{28,20},{32,40},... | collective-permute-start | bytes 1966088 | tf_op jit(solution)/shard_map/ppermute | solution.py:28
  56.0 0.6 collective-permute-start.22
  56.6 1.4 %collective-permute-done.20 = f32[24,4096]{1,0:T(8,128)S(1)} collective-permute-done((f32[24,4096]{1,0:T(8,128)S(1)}, f32[24,4096]{1,0:T(8,128)S(1)}, u32[]{:S(2)}, u32[]{:S(2)}) %collective-permute-start.20) | collective-permute-done | bytes 393248 | tf_op jit(solution)/shard_map/ppermute | solution.py:28
  58.1 1.5 %collective-permute-done.16 = f32[32,4096]{1,0:T(8,128)S(1)} collective-permute-done((f32[32,4096]{1,0:T(8,128)S(1)}, f32[32,4096]{1,0:T(8,128)S(1)}, u32[]{:S(2)}, u32[]{:S(2)}) %collective-permute-start.16) | collective-permute-done | bytes 524320 | tf_op jit(solution)/shard_map/ppermute | solution.py:24
  59.5 2.5 %collective-permute-start.23 = (f32[32,4096]{1,0:T(8,128)S(1)}, f32[32,4096]{1,0:T(8,128)S(1)}, u32[]{:S(2)}, u32[]{:S(2)}) collective-permute-start(f32[32,4096]{1,0:T(8,128)S(1)} %collective-permute-done.16), channel_id=1, source_target_pairs={{0,32},{4,228},{8,40},{12,236},{16,48},{20,244},{24,56},{28,252},{... | collective-permute-start | bytes 1572872 | tf_op jit(solution)/shard_map/ppermute | solution.py:24
  62.1 2.9 %collective-permute-done.14 = f32[40,4096]{1,0:T(8,128)S(1)} collective-permute-done((f32[40,4096]{1,0:T(8,128)S(1)}, f32[40,4096]{1,0:T(8,128)S(1)}, u32[]{:S(2)}, u32[]{:S(2)}) %collective-permute-start.14) | collective-permute-done | bytes 655392 | tf_op jit(solution)/shard_map/ppermute | solution.py:28
  65.4 1.6 %reduce-precision_convert_fusion = (bf16[4096,512]{1,0:T(8,128)(2,1)S(1)}, bf16[4096,512]{1,0:T(8,128)(2,1)S(1)}) fusion(f32[4096,256]{1,0:T(8,128)S(1)} %collective-permute-done.12, f32[4096,256]{1,0:T(8,128)S(1)} %copy-done.1, pred[4096]{0:T(1024)(128)(4,1)S(1)} %iota_compare_fusion.1), kind=kLoop, calls=%fused_computation.3 | loop fusion | flops 12582912 | bytes 16781312 | tf_op jit(solution)/shard_map/convert_element_type | solution.py:45
  67.0 2.0 %fusion.2 = f32[448,512]{1,0:T(8,128)S(1)} fusion(bf16[4096,512]{1,0:T(8,128)(2,1)S(1)} %get-tuple-element.19, bf16[224,4096]{1,0:T(8,128)(2,1)S(1)} %get-tuple-element.21, bf16[224,4096]{1,0:T(8,128)(2,1)S(1)} %get-tuple-element.22), kind=kOutput, calls=%fused_computation.11 | convolution fusion | flops 1886388224 | bytes 8781824 | tf_op jit(solution)/shard_map/dot_general | solution.py:79
  69.1 1.1 fusion.16
  70.2 2.0 %collective-permute-start.21 = (f32[40,4096]{1,0:T(8,128)S(1)}, f32[40,4096]{1,0:T(8,128)S(1)}, u32[]{:S(2)}, u32[]{:S(2)}) collective-permute-start(f32[40,4096]{1,0:T(8,128)S(1)} %collective-permute-done.14), channel_id=1, source_target_pairs={{0,8},{4,28},{8,16},{12,4},{16,24},{20,12},{24,0},{28,20},{32,40},... | collective-permute-start | bytes 1966088 | tf_op jit(solution)/shard_map/ppermute | solution.py:28
  72.2 1.2 fusion.12
  73.4 0.7 fusion.21
  75.2 1.3 %collective-permute-start.17 = (f32[352,128]{1,0:T(8,128)S(1)}, f32[352,128]{1,0:T(8,128)S(1)}, u32[]{:S(2)}, u32[]{:S(2)}) collective-permute-start(f32[352,128]{1,0:T(8,128)S(1)} %get-tuple-element.29), channel_id=1, source_target_pairs={{0,1},{1,2},{2,3},{3,0},{4,5},{5,6},{6,7},{7,4},{8,9},{9,10},{10,1... | collective-permute-start | bytes 540680 | tf_op jit(solution)/shard_map/ppermute | solution.py:36
  76.5 2.5 %collective-permute-start.19 = (f32[352,128]{1,0:T(8,128)S(1)}, f32[352,128]{1,0:T(8,128)S(1)}, u32[]{:S(2)}, u32[]{:S(2)}) collective-permute-start(f32[352,128]{1,0:T(8,128)S(1)} %get-tuple-element.30), channel_id=1, source_target_pairs={{0,2},{1,3},{2,0},{3,1},{4,6},{5,7},{6,4},{7,5},{8,10},{9,11},{10,... | collective-permute-start | bytes 540680 | tf_op jit(solution)/shard_map/ppermute | solution.py:36
  78.9 0.8 collective-permute-done.21
  79.7 2.5 %collective-permute-start.18 = (f32[352,128]{1,0:T(8,128)S(1)}, f32[352,128]{1,0:T(8,128)S(1)}, u32[]{:S(2)}, u32[]{:S(2)}) collective-permute-start(f32[352,128]{1,0:T(8,128)S(1)} %get-tuple-element.31), channel_id=1, source_target_pairs={{0,3},{1,0},{2,1},{3,2},{4,7},{5,4},{6,5},{7,6},{8,11},{9,8},{10,9... | collective-permute-start | bytes 540680 | tf_op jit(solution)/shard_map/ppermute | solution.py:36
  83.0 1.5 %fusion.7 = f32[320,512]{1,0:T(8,128)S(1)} fusion(bf16[4096,512]{1,0:T(8,128)(2,1)S(1)} %get-tuple-element.19, bf16[160,4096]{1,0:T(8,128)(2,1)S(1)} %get-tuple-element.23, bf16[160,4096]{1,0:T(8,128)(2,1)S(1)} %get-tuple-element.24), kind=kOutput, calls=%fused_computation.18 | convolution fusion | flops 1347420160 | bytes 7471104 | tf_op jit(solution)/shard_map/dot_general | solution.py:79
  84.6 0.9 fusion.17
  86.0 1.3 %collective-permute-start.25 = (f32[160,128]{1,0:T(8,128)S(1)}, f32[160,128]{1,0:T(8,128)S(1)}, u32[]{:S(2)}, u32[]{:S(2)}) collective-permute-start(f32[160,128]{1,0:T(8,128)S(1)} %get-tuple-element.45), channel_id=1, source_target_pairs={{0,1},{1,2},{2,3},{3,0},{4,5},{5,6},{6,7},{7,4},{8,9},{9,10},{10,1... | collective-permute-start | bytes 245768 | tf_op jit(solution)/shard_map/ppermute | solution.py:36
  87.3 2.4 %collective-permute-start.27 = (f32[160,128]{1,0:T(8,128)S(1)}, f32[160,128]{1,0:T(8,128)S(1)}, u32[]{:S(2)}, u32[]{:S(2)}) collective-permute-start(f32[160,128]{1,0:T(8,128)S(1)} %get-tuple-element.46), channel_id=1, source_target_pairs={{0,2},{1,3},{2,0},{3,1},{4,6},{5,7},{6,4},{7,5},{8,10},{9,11},{10,... | collective-permute-start | bytes 245768 | tf_op jit(solution)/shard_map/ppermute | solution.py:36
  89.7 1.2 collective-permute-start.26
  90.9 1.5 %collective-permute-done.27 = f32[160,128]{1,0:T(8,128)S(1)} collective-permute-done((f32[160,128]{1,0:T(8,128)S(1)}, f32[160,128]{1,0:T(8,128)S(1)}, u32[]{:S(2)}, u32[]{:S(2)}) %collective-permute-start.27) | collective-permute-done | bytes 81952 | tf_op jit(solution)/shard_map/ppermute | solution.py:36
  92.4 1.7 %collective-permute-done.26 = f32[160,128]{1,0:T(8,128)S(1)} collective-permute-done((f32[160,128]{1,0:T(8,128)S(1)}, f32[160,128]{1,0:T(8,128)S(1)}, u32[]{:S(2)}, u32[]{:S(2)}) %collective-permute-start.26) | collective-permute-done | bytes 81952 | tf_op jit(solution)/shard_map/ppermute | solution.py:36
  94.5 8.1 %collective-permute-start.28 = (f32[512,128]{1,0:T(8,128)S(1)}, f32[512,128]{1,0:T(8,128)S(1)}, u32[]{:S(2)}, u32[]{:S(2)}) collective-permute-start(f32[512,128]{1,0:T(8,128)S(1)} %fusion.20), channel_id=1, source_target_pairs={{0,4},{4,0},{8,12},{12,8},{16,20},{20,16},{24,28},{28,24},{32,36},... | collective-permute-start | bytes 786440 | tf_op jit(solution)/shard_map/ppermute | solution.py:32
  102.6 1.1 collective-permute-done.28
  103.8 0.6 gather_fusion.1
  104.4 21.4 %all_to_all.5 = f32[64,8,128]{2,1,0:T(8,128)S(1)} all-to-all(f32[64,8,128]{2,1,0:T(8,128)S(1)} %gather_fusion.1), channel_id=1, replica_groups=mesh['wide'=64,'narrow'=4] {'wide'}, dimensions={0} | all-to-all | bytes 524288 | tf_op jit(solution)/shard_map/all_to_all | solution.py:163
  125.9 0.9 copy.13
  (78 shorter events, 6.3 us)
Async XLA Ops:
  0.0 4.5 %copy-start = (s32[64]{0:T(128)S(1)}, s32[64]{0:T(128)}, u32[]{:S(2)}) copy-start(s32[64]{0:T(128)} %param.11) | copy-start | bytes 772
  0.0 5.9 %collective-permute-start = (f32[16,4096]{1,0:T(8,128)}, f32[16,4096]{1,0:T(8,128)S(1)}, u32[]{:S(2)}, u32[]{:S(2)}) collective-permute-start(f32[16,4096]{1,0:T(8,128)} %param.8), channel_id=1, source_target_pairs={{0,4},{4,0},{8,12},{12,8},{16,20},{20,16},{24,28},{28,24},{32,36},... | collective-permute-start | bytes 786440 | tf_op jit(solution)/shard_map/ppermute | solution.py:32
  6.0 59.5 %collective-permute-start.12 = (f32[4096,256]{1,0:T(8,128)}, f32[4096,256]{1,0:T(8,128)S(1)}, u32[]{:S(2)}, u32[]{:S(2)}) collective-permute-start(f32[4096,256]{1,0:T(8,128)} %param.9), channel_id=1, source_target_pairs={{0,4},{4,0},{8,12},{12,8},{16,20},{20,16},{24,28},{28,24},{32,36},... | collective-permute-start | bytes 12582920 | tf_op jit(solution)/shard_map/ppermute | solution.py:32
  7.2 6.8 %collective-permute-start.5 = (f32[16,4096]{1,0:T(8,128)S(1)}, f32[16,4096]{1,0:T(8,128)S(1)}, u32[]{:S(2)}, u32[]{:S(2)}) collective-permute-start(f32[16,4096]{1,0:T(8,128)S(1)} %pad_maximum_fusion.8), channel_id=1, source_target_pairs={{0,8},{4,28},{8,16},{12,4},{16,24},{20,12},{24,0},{28,20},{32,40},... | collective-permute-start | bytes 786440 | tf_op jit(solution)/shard_map/ppermute | solution.py:28
  8.3 9.0 %collective-permute-start.1 = (f32[16,4096]{1,0:T(8,128)S(1)}, f32[16,4096]{1,0:T(8,128)S(1)}, u32[]{:S(2)}, u32[]{:S(2)}) collective-permute-start(f32[16,4096]{1,0:T(8,128)S(1)} %pad_maximum_fusion.7), channel_id=1, source_target_pairs={{0,32},{4,228},{8,40},{12,236},{16,48},{20,244},{24,56},{28,252},{... | collective-permute-start | bytes 786440 | tf_op jit(solution)/shard_map/ppermute | solution.py:24
  14.0 7.0 %collective-permute-start.8 = (f32[8,4096]{1,0:T(8,128)S(1)}, f32[8,4096]{1,0:T(8,128)S(1)}, u32[]{:S(2)}, u32[]{:S(2)}) collective-permute-start(f32[8,4096]{1,0:T(8,128)S(1)} %constant_dynamic-slice_fusion), channel_id=1, source_target_pairs={{0,8},{4,28},{8,16},{12,4},{16,24},{20,12},{24,0},{28,20},{32,40},... | collective-permute-start | bytes 393224 | tf_op jit(solution)/shard_map/ppermute | solution.py:28
  17.3 36.6 %copy-start.2 = (f32[16,4096]{1,0:T(8,128)S(1)}, f32[16,4096]{1,0:T(8,128)}, u32[]{:S(2)}) copy-start(f32[16,4096]{1,0:T(8,128)} %param.8) | copy-start | bytes 786436
  17.3 22.5 %collective-permute-start.6 = (f32[24,4096]{1,0:T(8,128)S(1)}, f32[24,4096]{1,0:T(8,128)S(1)}, u32[]{:S(2)}, u32[]{:S(2)}) collective-permute-start(f32[24,4096]{1,0:T(8,128)S(1)} %pad_maximum_fusion.5), channel_id=1, source_target_pairs={{0,8},{4,28},{8,16},{12,4},{16,24},{20,12},{24,0},{28,20},{32,40},... | collective-permute-start | bytes 1179656 | tf_op jit(solution)/shard_map/ppermute | solution.py:28
  17.9 6.4 %collective-permute-start.2 = (f32[16,4096]{1,0:T(8,128)S(1)}, f32[16,4096]{1,0:T(8,128)S(1)}, u32[]{:S(2)}, u32[]{:S(2)}) collective-permute-start(f32[16,4096]{1,0:T(8,128)S(1)} %collective-permute-done.1), channel_id=1, source_target_pairs={{0,32},{4,228},{8,40},{12,236},{16,48},{20,244},{24,56},{28,252},{... | collective-permute-start | bytes 786440 | tf_op jit(solution)/shard_map/ppermute | solution.py:24
  21.1 18.8 %collective-permute-start.10 = (f32[32,4096]{1,0:T(8,128)S(1)}, f32[32,4096]{1,0:T(8,128)S(1)}, u32[]{:S(2)}, u32[]{:S(2)}) collective-permute-start(f32[32,4096]{1,0:T(8,128)S(1)} %pad_maximum_fusion.3), channel_id=1, source_target_pairs={{0,4},{4,0},{8,12},{12,8},{16,20},{20,16},{24,28},{28,24},{32,36},... | collective-permute-start | bytes 1572872 | tf_op jit(solution)/shard_map/ppermute | solution.py:32
  24.3 17.7 %collective-permute-start.9 = (f32[32,4096]{1,0:T(8,128)S(1)}, f32[32,4096]{1,0:T(8,128)S(1)}, u32[]{:S(2)}, u32[]{:S(2)}) collective-permute-start(f32[32,4096]{1,0:T(8,128)S(1)} %pad_maximum_fusion.3), channel_id=1, source_target_pairs={{0,32},{4,228},{8,40},{12,236},{16,48},{20,244},{24,56},{28,252},{... | collective-permute-start | bytes 1572872 | tf_op jit(solution)/shard_map/ppermute | solution.py:24
  27.7 8.9 %collective-permute-start.3 = (f32[16,4096]{1,0:T(8,128)S(1)}, f32[16,4096]{1,0:T(8,128)S(1)}, u32[]{:S(2)}, u32[]{:S(2)}) collective-permute-start(f32[16,4096]{1,0:T(8,128)S(1)} %collective-permute-done.2), channel_id=1, source_target_pairs={{0,32},{4,228},{8,40},{12,236},{16,48},{20,244},{24,56},{28,252},{... | collective-permute-start | bytes 786440 | tf_op jit(solution)/shard_map/ppermute | solution.py:24
  36.7 5.1 %collective-permute-start.4 = (f32[8,4096]{1,0:T(8,128)S(1)}, f32[8,4096]{1,0:T(8,128)S(1)}, u32[]{:S(2)}, u32[]{:S(2)}) collective-permute-start(f32[8,4096]{1,0:T(8,128)S(1)} %constant_dynamic-slice_fusion.1), channel_id=1, source_target_pairs={{0,32},{4,228},{8,40},{12,236},{16,48},{20,244},{24,56},{28,252},{... | collective-permute-start | bytes 393224 | tf_op jit(solution)/shard_map/ppermute | solution.py:24
  39.9 6.9 %collective-permute-start.13 = (f32[24,4096]{1,0:T(8,128)S(1)}, f32[24,4096]{1,0:T(8,128)S(1)}, u32[]{:S(2)}, u32[]{:S(2)}) collective-permute-start(f32[24,4096]{1,0:T(8,128)S(1)} %collective-permute-done.6), channel_id=1, source_target_pairs={{0,8},{4,28},{8,16},{12,4},{16,24},{20,12},{24,0},{28,20},{32,40},... | collective-permute-start | bytes 1179656 | tf_op jit(solution)/shard_map/ppermute | solution.py:28
  39.9 8.4 %collective-permute-start.11 = (f32[32,4096]{1,0:T(8,128)S(1)}, f32[32,4096]{1,0:T(8,128)S(1)}, u32[]{:S(2)}, u32[]{:S(2)}) collective-permute-start(f32[32,4096]{1,0:T(8,128)S(1)} %collective-permute-done.10), channel_id=1, source_target_pairs={{0,32},{4,228},{8,40},{12,236},{16,48},{20,244},{24,56},{28,252},{... | collective-permute-start | bytes 1572872 | tf_op jit(solution)/shard_map/ppermute | solution.py:24
  41.9 12.0 %collective-permute-start.7 = (f32[40,4096]{1,0:T(8,128)S(1)}, f32[40,4096]{1,0:T(8,128)S(1)}, u32[]{:S(2)}, u32[]{:S(2)}) collective-permute-start(f32[40,4096]{1,0:T(8,128)S(1)} %pad_maximum_fusion.2), channel_id=1, source_target_pairs={{0,8},{4,28},{8,16},{12,4},{16,24},{20,12},{24,0},{28,20},{32,40},... | collective-permute-start | bytes 1966088 | tf_op jit(solution)/shard_map/ppermute | solution.py:28
  42.0 14.0 %collective-permute-start.15 = (f32[32,4096]{1,0:T(8,128)S(1)}, f32[32,4096]{1,0:T(8,128)S(1)}, u32[]{:S(2)}, u32[]{:S(2)}) collective-permute-start(f32[32,4096]{1,0:T(8,128)S(1)} %collective-permute-done.9), channel_id=1, source_target_pairs={{0,32},{4,228},{8,40},{12,236},{16,48},{20,244},{24,56},{28,252},{... | collective-permute-start | bytes 1572872 | tf_op jit(solution)/shard_map/ppermute | solution.py:24
  46.8 11.2 %collective-permute-start.20 = (f32[24,4096]{1,0:T(8,128)S(1)}, f32[24,4096]{1,0:T(8,128)S(1)}, u32[]{:S(2)}, u32[]{:S(2)}) collective-permute-start(f32[24,4096]{1,0:T(8,128)S(1)} %collective-permute-done.13), channel_id=1, source_target_pairs={{0,8},{4,28},{8,16},{12,4},{16,24},{20,12},{24,0},{28,20},{32,40},... | collective-permute-start | bytes 1179656 | tf_op jit(solution)/shard_map/ppermute | solution.py:28
  48.3 11.2 %collective-permute-start.16 = (f32[32,4096]{1,0:T(8,128)S(1)}, f32[32,4096]{1,0:T(8,128)S(1)}, u32[]{:S(2)}, u32[]{:S(2)}) collective-permute-start(f32[32,4096]{1,0:T(8,128)S(1)} %collective-permute-done.11), channel_id=1, source_target_pairs={{0,32},{4,228},{8,40},{12,236},{16,48},{20,244},{24,56},{28,252},{... | collective-permute-start | bytes 1572872 | tf_op jit(solution)/shard_map/ppermute | solution.py:24
  54.7 10.7 %copy-start.1 = (f32[4096,256]{1,0:T(8,128)S(1)}, f32[4096,256]{1,0:T(8,128)}, u32[]{:S(2)}) copy-start(f32[4096,256]{1,0:T(8,128)} %param.9) | copy-start | bytes 12582916
  54.7 10.3 %collective-permute-start.14 = (f32[40,4096]{1,0:T(8,128)S(1)}, f32[40,4096]{1,0:T(8,128)S(1)}, u32[]{:S(2)}, u32[]{:S(2)}) collective-permute-start(f32[40,4096]{1,0:T(8,128)S(1)} %collective-permute-done.7), channel_id=1, source_target_pairs={{0,8},{4,28},{8,16},{12,4},{16,24},{20,12},{24,0},{28,20},{32,40},... | collective-permute-start | bytes 1966088 | tf_op jit(solution)/shard_map/ppermute | solution.py:28
  56.0 18.2 %collective-permute-start.22 = (f32[32,4096]{1,0:T(8,128)S(1)}, f32[32,4096]{1,0:T(8,128)S(1)}, u32[]{:S(2)}, u32[]{:S(2)}) collective-permute-start(f32[32,4096]{1,0:T(8,128)S(1)} %collective-permute-done.15), channel_id=1, source_target_pairs={{0,32},{4,228},{8,40},{12,236},{16,48},{20,244},{24,56},{28,252},{... | collective-permute-start | bytes 1572872 | tf_op jit(solution)/shard_map/ppermute | solution.py:24
  59.5 22.7 %collective-permute-start.23 = (f32[32,4096]{1,0:T(8,128)S(1)}, f32[32,4096]{1,0:T(8,128)S(1)}, u32[]{:S(2)}, u32[]{:S(2)}) collective-permute-start(f32[32,4096]{1,0:T(8,128)S(1)} %collective-permute-done.16), channel_id=1, source_target_pairs={{0,32},{4,228},{8,40},{12,236},{16,48},{20,244},{24,56},{28,252},{... | collective-permute-start | bytes 1572872 | tf_op jit(solution)/shard_map/ppermute | solution.py:24
  70.2 9.5 %collective-permute-start.21 = (f32[40,4096]{1,0:T(8,128)S(1)}, f32[40,4096]{1,0:T(8,128)S(1)}, u32[]{:S(2)}, u32[]{:S(2)}) collective-permute-start(f32[40,4096]{1,0:T(8,128)S(1)} %collective-permute-done.14), channel_id=1, source_target_pairs={{0,8},{4,28},{8,16},{12,4},{16,24},{20,12},{24,0},{28,20},{32,40},... | collective-permute-start | bytes 1966088 | tf_op jit(solution)/shard_map/ppermute | solution.py:28
  74.2 8.4 %collective-permute-start.24 = (f32[32,4096]{1,0:T(8,128)S(1)}, f32[32,4096]{1,0:T(8,128)S(1)}, u32[]{:S(2)}, u32[]{:S(2)}) collective-permute-start(f32[32,4096]{1,0:T(8,128)S(1)} %collective-permute-done.22), channel_id=1, source_target_pairs={{0,32},{4,228},{8,40},{12,236},{16,48},{20,244},{24,56},{28,252},{... | collective-permute-start | bytes 1572872 | tf_op jit(solution)/shard_map/ppermute | solution.py:24
  75.2 14.5 %collective-permute-start.17 = (f32[352,128]{1,0:T(8,128)S(1)}, f32[352,128]{1,0:T(8,128)S(1)}, u32[]{:S(2)}, u32[]{:S(2)}) collective-permute-start(f32[352,128]{1,0:T(8,128)S(1)} %get-tuple-element.29), channel_id=1, source_target_pairs={{0,1},{1,2},{2,3},{3,0},{4,5},{5,6},{6,7},{7,4},{8,9},{9,10},{10,1... | collective-permute-start | bytes 540680 | tf_op jit(solution)/shard_map/ppermute | solution.py:36
  76.5 14.4 %collective-permute-start.19 = (f32[352,128]{1,0:T(8,128)S(1)}, f32[352,128]{1,0:T(8,128)S(1)}, u32[]{:S(2)}, u32[]{:S(2)}) collective-permute-start(f32[352,128]{1,0:T(8,128)S(1)} %get-tuple-element.30), channel_id=1, source_target_pairs={{0,2},{1,3},{2,0},{3,1},{4,6},{5,7},{6,4},{7,5},{8,10},{9,11},{10,... | collective-permute-start | bytes 540680 | tf_op jit(solution)/shard_map/ppermute | solution.py:36
  79.7 11.1 %collective-permute-start.18 = (f32[352,128]{1,0:T(8,128)S(1)}, f32[352,128]{1,0:T(8,128)S(1)}, u32[]{:S(2)}, u32[]{:S(2)}) collective-permute-start(f32[352,128]{1,0:T(8,128)S(1)} %get-tuple-element.31), channel_id=1, source_target_pairs={{0,3},{1,0},{2,1},{3,2},{4,7},{5,4},{6,5},{7,6},{8,11},{9,8},{10,9... | collective-permute-start | bytes 540680 | tf_op jit(solution)/shard_map/ppermute | solution.py:36
  86.0 5.0 %collective-permute-start.25 = (f32[160,128]{1,0:T(8,128)S(1)}, f32[160,128]{1,0:T(8,128)S(1)}, u32[]{:S(2)}, u32[]{:S(2)}) collective-permute-start(f32[160,128]{1,0:T(8,128)S(1)} %get-tuple-element.45), channel_id=1, source_target_pairs={{0,1},{1,2},{2,3},{3,0},{4,5},{5,6},{6,7},{7,4},{8,9},{9,10},{10,1... | collective-permute-start | bytes 245768 | tf_op jit(solution)/shard_map/ppermute | solution.py:36
  87.3 5.1 %collective-permute-start.27 = (f32[160,128]{1,0:T(8,128)S(1)}, f32[160,128]{1,0:T(8,128)S(1)}, u32[]{:S(2)}, u32[]{:S(2)}) collective-permute-start(f32[160,128]{1,0:T(8,128)S(1)} %get-tuple-element.46), channel_id=1, source_target_pairs={{0,2},{1,3},{2,0},{3,1},{4,6},{5,7},{6,4},{7,5},{8,10},{9,11},{10,... | collective-permute-start | bytes 245768 | tf_op jit(solution)/shard_map/ppermute | solution.py:36
  89.7 4.4 %collective-permute-start.26 = (f32[160,128]{1,0:T(8,128)S(1)}, f32[160,128]{1,0:T(8,128)S(1)}, u32[]{:S(2)}, u32[]{:S(2)}) collective-permute-start(f32[160,128]{1,0:T(8,128)S(1)} %get-tuple-element.47), channel_id=1, source_target_pairs={{0,3},{1,0},{2,1},{3,2},{4,7},{5,4},{6,5},{7,6},{8,11},{9,8},{10,9... | collective-permute-start | bytes 245768 | tf_op jit(solution)/shard_map/ppermute | solution.py:36
  94.5 9.2 %collective-permute-start.28 = (f32[512,128]{1,0:T(8,128)S(1)}, f32[512,128]{1,0:T(8,128)S(1)}, u32[]{:S(2)}, u32[]{:S(2)}) collective-permute-start(f32[512,128]{1,0:T(8,128)S(1)} %fusion.20), channel_id=1, source_target_pairs={{0,4},{4,0},{8,12},{12,8},{16,20},{20,16},{24,28},{28,24},{32,36},... | collective-permute-start | bytes 786440 | tf_op jit(solution)/shard_map/ppermute | solution.py:32

commit v4 on v3

--- a/solution.py
+++ b/solution.py
@@ -54,7 +54,9 @@
     width = stored_amps.shape[1]
 
     sibling = other_core(stored_amps)
-    theirs = other_core(after(integrals, sibling))
+    theirs = jnp.concatenate(
+        [other_core(after(part, sibling)) for part in jnp.split(integrals, 4)], axis=0
+    )
     top, low = stored_amps[:BR], stored_amps[BR:]
 
     def by_core(mine, others):
@@ -105,8 +107,8 @@
     s2 = along_y(s1)
     near = times([first, second, f1, s1, row_own, by_core(a1, b1)])
     a3 = along_z(a2)
-    b3 = along_z(b2)
-    s3 = along_y(after(s2, near))
+    b3 = along_z(after(b2, near))
+    s3 = along_y(after(s2, a2, b2))
     middle = times([f2, s2, by_core(a2, b2)])
     a4 = along_z(after(a3, middle))
     span = NX * G

time: 127 us -> 155 us (1.22)
  waiting for transfers between devices: 31.8 us -> 46.5 us
  other arithmetic: 6.41 us -> 14 us
  local copies, waits for them, and re-layouts: 4.14 us -> 11.1 us
  starting transfers between devices: 55 us -> 52.5 us
    ppermute x11, starting transfers between devices: 24.8 us -> 16.1 us  [along_z(): return lax.ppermute(block, 'wide', wide_pairs(1, 0))]
    ppermute x8, waiting for transfers between devices: 9.74 us -> 18 us  [along_y(): return lax.ppermute(block, 'wide', wide_pairs(0, 1))]
    ppermute x11, waiting for transfers between devices: 17.7 us -> 24.9 us  [along_z(): return lax.ppermute(block, 'wide', wide_pairs(1, 0))]
    convert_element_type x4, other arithmetic: 2.99 us -> 9.18 us  [halves(): return (high.astype(jnp.bfloat16), (block - high).astype(jnp.bfloat16))]
    ppermute x8, starting transfers between devices: 7.03 us -> 12.1 us  [along_y(): return lax.ppermute(block, 'wide', wide_pairs(0, 1))]
    unnamed x18 -> x28, local copies, waits for them, and re-layouts: 1.13 us -> 5.5 us
    split x0 -> x1, local copies, waits for them, and re-layouts: none -> 2.53 us  [on_device(): jnp.split(integrals, 4)]
    ppermute x4 -> x7, starting transfers between devices: 12.1 us -> 13.5 us  [other_core(): return lax.ppermute(block, 'wide', wide_pairs(0, 0, True))]
  transfers between devices with their start and end apart: 29 -> 32, of which waited for: 15 -> 16; matrix products, arithmetic and copies ran while one was open for 13% -> 18% of each run, Pallas kernels for 0% -> 0%
where the time goes in v4:
time: 155 us
  starting transfers between devices  52.5 us (34%)
  waiting for transfers between devices  46.5 us (30%)
  blocking collectives  22.6 us (15%)
  other arithmetic  14 us (9%)
  local copies, waits for them, and re-layouts  11.1 us (7%)
  matrix products  7.55 us (5%)
    ppermute x11, waiting for transfers between devices, along_z(): return lax.ppermute(block, 'wide', wide_pairs(1, 0))  24.9 us
    all_to_all x1, blocking collectives, on_device(): got = lax.all_to_all(sent, 'wide', split_axis=0, concat_axis=0, tiled=True)  22.6 us
    ppermute x8, waiting for transfers between devices, along_y(): return lax.ppermute(block, 'wide', wide_pairs(0, 1))  18 us
    ppermute x11, starting transfers between devices, along_z(): return lax.ppermute(block, 'wide', wide_pairs(1, 0))  16.1 us
    ppermute x7, starting transfers between devices, other_core(): return lax.ppermute(block, 'wide', wide_pairs(0, 0, True))  13.5 us
    ppermute x8, starting transfers between devices, along_y(): return lax.ppermute(block, 'wide', wide_pairs(0, 1))  12.1 us
    ppermute x6, starting transfers between devices, along_x(): lax.ppermute(block, 'narrow', [(i, (i + step) % NX) for i in range(NX)])  10.9 us
    convert_element_type x4, other arithmetic, halves(): return (high.astype(jnp.bfloat16), (block - high).astype(jnp.bfloat16))  9.18 us
  transfers between devices with their start and end apart: 32, of which 16 were waited for; matrix products, arithmetic and copies ran while one was open for 18% of the time, Pallas kernels for 0%

profile of v4, /device:TPU:1, one launch (start us, length us, event | category | flops | bytes accessed | tf_op | source)
XLA Modules:
  0.0 154.7 jit_solution(598138765547632059)
XLA Ops:
  0.0 3.2 %collective-permute-start = (f32[16,4096]{1,0:T(8,128)}, f32[16,4096]{1,0:T(8,128)S(1)}, u32[]{:S(2)}, u32[]{:S(2)}) collective-permute-start(f32[16,4096]{1,0:T(8,128)} %param.8), channel_id=1, source_target_pairs={{0,4},{4,0},{8,12},{12,8},{16,20},{20,16},{24,28},{28,24},{32,36},... | collective-permute-start | bytes 786440 | tf_op jit(solution)/shard_map/ppermute | solution.py:32
  3.3 1.2 dynamic_slice.37
  6.0 2.5 %fusion.52 = (f32[1024,256]{1,0:T(8,128)S(1)}, f32[1024,256]{1,0:T(8,128)S(1)}, f32[1024,256]{1,0:T(8,128)S(1)}, f32[1024,256]{1,0:T(8,128)S(1)}) fusion(f32[4096,256]{1,0:T(8,128)} %param.9), kind=kLoop, calls=%fused_computation.208 | loop fusion | bytes 8388608 | tf_op jit(solution)/shard_map/split | solution.py:58
  9.3 3.9 %collective-permute-start.1 = (f32[16,4096]{1,0:T(8,128)S(1)}, f32[16,4096]{1,0:T(8,128)S(1)}, u32[]{:S(2)}, u32[]{:S(2)}) collective-permute-start(f32[16,4096]{1,0:T(8,128)S(1)} %pad_maximum_fusion.7), channel_id=1, source_target_pairs={{0,32},{4,228},{8,40},{12,236},{16,48},{20,244},{24,56},{28,252},{... | collective-permute-start | bytes 786440 | tf_op jit(solution)/shard_map/ppermute | solution.py:24
  13.3 2.8 %collective-permute-start.5 = (f32[16,4096]{1,0:T(8,128)S(1)}, f32[16,4096]{1,0:T(8,128)S(1)}, u32[]{:S(2)}, u32[]{:S(2)}) collective-permute-start(f32[16,4096]{1,0:T(8,128)S(1)} %pad_maximum_fusion.8), channel_id=1, source_target_pairs={{0,8},{4,28},{8,16},{12,4},{16,24},{20,12},{24,0},{28,20},{32,40},... | collective-permute-start | bytes 786440 | tf_op jit(solution)/shard_map/ppermute | solution.py:28
  16.6 2.8 %collective-permute-done.5 = f32[16,4096]{1,0:T(8,128)S(1)} collective-permute-done((f32[16,4096]{1,0:T(8,128)S(1)}, f32[16,4096]{1,0:T(8,128)S(1)}, u32[]{:S(2)}, u32[]{:S(2)}) %collective-permute-start.5) | collective-permute-done | bytes 262176 | tf_op jit(solution)/shard_map/ppermute | solution.py:28
  19.4 3.1 %collective-permute-start.6 = (f32[24,4096]{1,0:T(8,128)S(1)}, f32[24,4096]{1,0:T(8,128)}, u32[]{:S(2)}, u32[]{:S(2)}) collective-permute-start(f32[24,4096]{1,0:T(8,128)S(1)} %pad_maximum_fusion.5), channel_id=1, source_target_pairs={{0,8},{4,28},{8,16},{12,4},{16,24},{20,12},{24,0},{28,20},{32,40},... | collective-permute-start | bytes 1179656 | tf_op jit(solution)/shard_map/ppermute | solution.py:28
  23.3 4.4 %collective-permute-done.2 = f32[16,4096]{1,0:T(8,128)S(1)} collective-permute-done((f32[16,4096]{1,0:T(8,128)S(1)}, f32[16,4096]{1,0:T(8,128)S(1)}, u32[]{:S(2)}, u32[]{:S(2)}) %collective-permute-start.2) | collective-permute-done | bytes 262176 | tf_op jit(solution)/shard_map/ppermute | solution.py:24
  27.8 2.3 %collective-permute-start.3 = (f32[16,4096]{1,0:T(8,128)S(1)}, f32[16,4096]{1,0:T(8,128)S(1)}, u32[]{:S(2)}, u32[]{:S(2)}) collective-permute-start(f32[16,4096]{1,0:T(8,128)S(1)} %collective-permute-done.2), channel_id=1, source_target_pairs={{0,32},{4,228},{8,40},{12,236},{16,48},{20,244},{24,56},{28,252},{... | collective-permute-start | bytes 786440 | tf_op jit(solution)/shard_map/ppermute | solution.py:24
  30.1 3.3 %collective-permute-done.3 = f32[16,4096]{1,0:T(8,128)S(1)} collective-permute-done((f32[16,4096]{1,0:T(8,128)S(1)}, f32[16,4096]{1,0:T(8,128)S(1)}, u32[]{:S(2)}, u32[]{:S(2)}) %collective-permute-start.3) | collective-permute-done | bytes 262176 | tf_op jit(solution)/shard_map/ppermute | solution.py:24
  33.4 3.2 %collective-permute-start.4 = (f32[8,4096]{1,0:T(8,128)S(1)}, f32[8,4096]{1,0:T(8,128)S(1)}, u32[]{:S(2)}, u32[]{:S(2)}) collective-permute-start(f32[8,4096]{1,0:T(8,128)S(1)} %constant_dynamic-slice_fusion.1), channel_id=1, source_target_pairs={{0,32},{4,228},{8,40},{12,236},{16,48},{20,244},{24,56},{28,252},{... | collective-permute-start | bytes 393224 | tf_op jit(solution)/shard_map/ppermute | solution.py:24
  36.7 1.8 %collective-permute-done.4 = f32[8,4096]{1,0:T(8,128)S(1)} collective-permute-done((f32[8,4096]{1,0:T(8,128)S(1)}, f32[8,4096]{1,0:T(8,128)S(1)}, u32[]{:S(2)}, u32[]{:S(2)}) %collective-permute-start.4) | collective-permute-done | bytes 131104 | tf_op jit(solution)/shard_map/ppermute | solution.py:24
  38.7 1.0 constant_dynamic-update-slice_fusion.4
  39.7 8.7 %collective-permute-done.7 = f32[40,4096]{1,0:T(8,128)S(1)} collective-permute-done((f32[40,4096]{1,0:T(8,128)S(1)}, f32[40,4096]{1,0:T(8,128)S(1)}, u32[]{:S(2)}, u32[]{:S(2)}) %collective-permute-start.7) | collective-permute-done | bytes 655392 | tf_op jit(solution)/shard_map/ppermute | solution.py:28
  48.4 0.9 collective-permute-start.8
  49.4 3.1 %collective-permute-done.8 = f32[8,4096]{1,0:T(8,128)S(1)} collective-permute-done((f32[8,4096]{1,0:T(8,128)S(1)}, f32[8,4096]{1,0:T(8,128)S(1)}, u32[]{:S(2)}, u32[]{:S(2)}) %collective-permute-start.8) | collective-permute-done | bytes 131104 | tf_op jit(solution)/shard_map/ppermute | solution.py:28
  52.5 1.8 %collective-permute-start.16 = (f32[24,4096]{1,0:T(8,128)}, f32[24,4096]{1,0:T(8,128)}, u32[]{:S(2)}, u32[]{:S(2)}) collective-permute-start(f32[24,4096]{1,0:T(8,128)} %collective-permute-done.6), channel_id=1, source_target_pairs={{0,8},{4,28},{8,16},{12,4},{16,24},{20,12},{24,0},{28,20},{32,40},... | collective-permute-start | bytes 1179656 | tf_op jit(solution)/shard_map/ppermute | solution.py:28
  55.2 5.2 %collective-permute-start.10 = (f32[32,4096]{1,0:T(8,128)}, f32[32,4096]{1,0:T(8,128)}, u32[]{:S(2)}, u32[]{:S(2)}) collective-permute-start(f32[32,4096]{1,0:T(8,128)} %pad_maximum_fusion.3), channel_id=1, source_target_pairs={{0,4},{4,0},{8,12},{12,8},{16,20},{20,16},{24,28},{28,24},{32,36},... | collective-permute-start | bytes 1572872 | tf_op jit(solution)/shard_map/ppermute | solution.py:32
  60.4 1.0 copy-done.4
  61.5 1.0 copy-done.5
  62.4 4.8 %reduce-precision_convert_fusion = (bf16[4096,512]{1,0:T(8,128)(2,1)S(1)}, bf16[4096,512]{1,0:T(8,128)(2,1)S(1)}) fusion(f32[1024,256]{1,0:T(8,128)} %copy-done.3, f32[1024,256]{1,0:T(8,128)} %copy-done.5, f32[1024,256]{1,0:T(8,128)} %copy-done.4, f32[1024,256]{1,0:T(8,128)} %collective-permute-done.12, f32[4096,256]{1,0:T(8,128)S(1)} %copy-done.1, ...), kind=kLoop, calls=%fused_computation.3 | loop fusion | flops 18874368 | bytes 16781312 | tf_op jit(solution)/shard_map/convert_element_type | solution.py:45
  67.2 3.0 %collective-permute-start.23 = (f32[24,4096]{1,0:T(8,128)}, f32[24,4096]{1,0:T(8,128)S(1)}, u32[]{:S(2)}, u32[]{:S(2)}) collective-permute-start(f32[24,4096]{1,0:T(8,128)} %collective-permute-done.16), channel_id=1, source_target_pairs={{0,8},{4,28},{8,16},{12,4},{16,24},{20,12},{24,0},{28,20},{32,40},... | collective-permute-start | bytes 1179656 | tf_op jit(solution)/shard_map/ppermute | solution.py:28
  71.8 3.5 %collective-permute-done.23 = f32[24,4096]{1,0:T(8,128)S(1)} collective-permute-done((f32[24,4096]{1,0:T(8,128)}, f32[24,4096]{1,0:T(8,128)S(1)}, u32[]{:S(2)}, u32[]{:S(2)}) %collective-permute-start.23) | collective-permute-done | bytes 393248 | tf_op jit(solution)/shard_map/ppermute | solution.py:28
  75.3 3.5 %collective-permute-done.9 = f32[32,4096]{1,0:T(8,128)S(1)} collective-permute-done((f32[32,4096]{1,0:T(8,128)}, f32[32,4096]{1,0:T(8,128)S(1)}, u32[]{:S(2)}, u32[]{:S(2)}) %collective-permute-start.9) | collective-permute-done | bytes 524320 | tf_op jit(solution)/shard_map/ppermute | solution.py:24
  78.8 1.2 collective-permute-start.18
  80.0 4.4 %collective-permute-done.11 = f32[32,4096]{1,0:T(8,128)S(1)} collective-permute-done((f32[32,4096]{1,0:T(8,128)}, f32[32,4096]{1,0:T(8,128)S(1)}, u32[]{:S(2)}, u32[]{:S(2)}) %collective-permute-start.11) | collective-permute-done | bytes 524320 | tf_op jit(solution)/shard_map/ppermute | solution.py:24
  86.1 2.6 %fusion.1 = (bf16[224,4096]{1,0:T(8,128)(2,1)S(1)}, bf16[224,4096]{1,0:T(8,128)(2,1)S(1)}) fusion(f32[224,4096]{1,0:T(8,128)} %select_dynamic-update-slice_fusion.2), kind=kLoop, calls=%fused_computation.10 | loop fusion | flops 3670016 | bytes 7340032 | tf_op jit(solution)/shard_map/convert_element_type | solution.py:45
  88.7 1.0 collective-permute-start.19
  89.7 2.0 %fusion.2 = f32[448,512]{1,0:T(8,128)S(1)} fusion(bf16[4096,512]{1,0:T(8,128)(2,1)S(1)} %get-tuple-element.27, bf16[224,4096]{1,0:T(8,128)(2,1)S(1)} %get-tuple-element.33, bf16[224,4096]{1,0:T(8,128)(2,1)S(1)} %get-tuple-element.34), kind=kOutput, calls=%fused_computation.11 | convolution fusion | flops 1886388224 | bytes 8781824 | tf_op jit(solution)/shard_map/dot_general | solution.py:81
  91.9 1.1 fusion.16
  93.0 4.1 %collective-permute-done.19 = f32[32,4096]{1,0:T(8,128)S(1)} collective-permute-done((f32[32,4096]{1,0:T(8,128)S(1)}, f32[32,4096]{1,0:T(8,128)S(1)}, u32[]{:S(2)}, u32[]{:S(2)}) %collective-permute-start.19) | collective-permute-done | bytes 524320 | tf_op jit(solution)/shard_map/ppermute | solution.py:24
  97.1 1.8 %collective-permute-start.26 = (f32[32,4096]{1,0:T(8,128)S(1)}, f32[32,4096]{1,0:T(8,128)S(1)}, u32[]{:S(2)}, u32[]{:S(2)}) collective-permute-start(f32[32,4096]{1,0:T(8,128)S(1)} %collective-permute-done.19), channel_id=1, source_target_pairs={{0,32},{4,228},{8,40},{12,236},{16,48},{20,244},{24,56},{28,252},{... | collective-permute-start | bytes 1572872 | tf_op jit(solution)/shard_map/ppermute | solution.py:24
  99.1 1.3 fusion.11
  100.5 1.2 fusion.12
  102.7 1.8 %collective-permute-start.27 = (f32[32,4096]{1,0:T(8,128)S(1)}, f32[32,4096]{1,0:T(8,128)S(1)}, u32[]{:S(2)}, u32[]{:S(2)}) collective-permute-start(f32[32,4096]{1,0:T(8,128)S(1)} %collective-permute-done.25), channel_id=1, source_target_pairs={{0,32},{4,228},{8,40},{12,236},{16,48},{20,244},{24,56},{28,252},{... | collective-permute-start | bytes 1572872 | tf_op jit(solution)/shard_map/ppermute | solution.py:24
  105.2 1.3 collective-permute-start.20
  106.5 2.5 %collective-permute-start.22 = (f32[352,128]{1,0:T(8,128)S(1)}, f32[352,128]{1,0:T(8,128)S(1)}, u32[]{:S(2)}, u32[]{:S(2)}) collective-permute-start(f32[352,128]{1,0:T(8,128)S(1)} %get-tuple-element.42), channel_id=1, source_target_pairs={{0,2},{1,3},{2,0},{3,1},{4,6},{5,7},{6,4},{7,5},{8,10},{9,11},{10,... | collective-permute-start | bytes 540680 | tf_op jit(solution)/shard_map/ppermute | solution.py:36
  108.9 2.2 %collective-permute-start.21 = (f32[352,128]{1,0:T(8,128)S(1)}, f32[352,128]{1,0:T(8,128)S(1)}, u32[]{:S(2)}, u32[]{:S(2)}) collective-permute-start(f32[352,128]{1,0:T(8,128)S(1)} %get-tuple-element.43), channel_id=1, source_target_pairs={{0,3},{1,0},{2,1},{3,2},{4,7},{5,4},{6,5},{7,6},{8,11},{9,8},{10,9... | collective-permute-start | bytes 540680 | tf_op jit(solution)/shard_map/ppermute | solution.py:36
  111.4 2.6 %collective-permute-done.27 = f32[32,4096]{1,0:T(8,128)S(1)} collective-permute-done((f32[32,4096]{1,0:T(8,128)S(1)}, f32[32,4096]{1,0:T(8,128)S(1)}, u32[]{:S(2)}, u32[]{:S(2)}) %collective-permute-start.27) | collective-permute-done | bytes 524320 | tf_op jit(solution)/shard_map/ppermute | solution.py:24
  114.5 1.6 %fusion.7 = f32[320,512]{1,0:T(8,128)S(1)} fusion(bf16[4096,512]{1,0:T(8,128)(2,1)S(1)} %get-tuple-element.27, bf16[160,4096]{1,0:T(8,128)(2,1)S(1)} %get-tuple-element.35, bf16[160,4096]{1,0:T(8,128)(2,1)S(1)} %get-tuple-element.36), kind=kOutput, calls=%fused_computation.18 | convolution fusion | flops 1347420160 | bytes 7471104 | tf_op jit(solution)/shard_map/dot_general | solution.py:81
  117.4 1.3 collective-permute-start.28
  118.7 2.4 %collective-permute-start.30 = (f32[160,128]{1,0:T(8,128)S(1)}, f32[160,128]{1,0:T(8,128)S(1)}, u32[]{:S(2)}, u32[]{:S(2)}) collective-permute-start(f32[160,128]{1,0:T(8,128)S(1)} %get-tuple-element.58), channel_id=1, source_target_pairs={{0,2},{1,3},{2,0},{3,1},{4,6},{5,7},{6,4},{7,5},{8,10},{9,11},{10,... | collective-permute-start | bytes 245768 | tf_op jit(solution)/shard_map/ppermute | solution.py:36
  121.1 1.2 collective-permute-start.29
  122.3 1.5 collective-permute-done.30
  123.8 0.9 collective-permute-done.29
  125.0 4.2 %collective-permute-start.31 = (f32[512,128]{1,0:T(8,128)S(1)}, f32[512,128]{1,0:T(8,128)S(1)}, u32[]{:S(2)}, u32[]{:S(2)}) collective-permute-start(f32[512,128]{1,0:T(8,128)S(1)} %fusion.20), channel_id=1, source_target_pairs={{0,4},{4,0},{8,12},{12,8},{16,20},{20,16},{24,28},{28,24},{32,36},... | collective-permute-start | bytes 786440 | tf_op jit(solution)/shard_map/ppermute | solution.py:32
  129.3 1.1 collective-permute-done.31
  131.1 22.6 %all_to_all.5 = f32[64,8,128]{2,1,0:T(8,128)S(1)} all-to-all(f32[64,8,128]{2,1,0:T(8,128)S(1)} %gather_fusion.1), channel_id=1, replica_groups=mesh['wide'=64,'narrow'=4] {'wide'}, dimensions={0} | all-to-all | bytes 524288 | tf_op jit(solution)/shard_map/all_to_all | solution.py:165
  (95 shorter events, 13.9 us)
Async XLA Ops:
  0.0 5.2 %copy-start = (s32[64]{0:T(128)S(1)}, s32[64]{0:T(128)}, u32[]{:S(2)}) copy-start(s32[64]{0:T(128)} %param.11) | copy-start | bytes 772
  0.0 8.5 %collective-permute-start = (f32[16,4096]{1,0:T(8,128)}, f32[16,4096]{1,0:T(8,128)S(1)}, u32[]{:S(2)}, u32[]{:S(2)}) collective-permute-start(f32[16,4096]{1,0:T(8,128)} %param.8), channel_id=1, source_target_pairs={{0,4},{4,0},{8,12},{12,8},{16,20},{20,16},{24,28},{28,24},{32,36},... | collective-permute-start | bytes 786440 | tf_op jit(solution)/shard_map/ppermute | solution.py:32
  6.0 3.3 %copy-start.7 = (f32[16,4096]{1,0:T(8,128)S(1)}, f32[16,4096]{1,0:T(8,128)}, u32[]{:S(2)}) copy-start(f32[16,4096]{1,0:T(8,128)} %param.8) | copy-start | bytes 786436
  8.5 46.6 %collective-permute-start.15 = (f32[1024,256]{1,0:T(8,128)S(1)}, f32[1024,256]{1,0:T(8,128)S(1)}, u32[]{:S(2)}, u32[]{:S(2)}) collective-permute-start(f32[1024,256]{1,0:T(8,128)S(1)} %get-tuple-element.22), channel_id=1, source_target_pairs={{0,4},{4,0},{8,12},{12,8},{16,20},{20,16},{24,28},{28,24},{32,36},... | collective-permute-start | bytes 3145736 | tf_op jit(solution)/shard_map/ppermute | solution.py:32
  8.7 51.7 %collective-permute-start.13 = (f32[1024,256]{1,0:T(8,128)S(1)}, f32[1024,256]{1,0:T(8,128)S(1)}, u32[]{:S(2)}, u32[]{:S(2)}) collective-permute-start(f32[1024,256]{1,0:T(8,128)S(1)} %get-tuple-element.20), channel_id=1, source_target_pairs={{0,4},{4,0},{8,12},{12,8},{16,20},{20,16},{24,28},{28,24},{32,36},... | collective-permute-start | bytes 3145736 | tf_op jit(solution)/shard_map/ppermute | solution.py:32
  9.1 51.2 %collective-permute-start.14 = (f32[1024,256]{1,0:T(8,128)S(1)}, f32[1024,256]{1,0:T(8,128)S(1)}, u32[]{:S(2)}, u32[]{:S(2)}) collective-permute-start(f32[1024,256]{1,0:T(8,128)S(1)} %get-tuple-element.21), channel_id=1, source_target_pairs={{0,4},{4,0},{8,12},{12,8},{16,20},{20,16},{24,28},{28,24},{32,36},... | collective-permute-start | bytes 3145736 | tf_op jit(solution)/shard_map/ppermute | solution.py:32
  9.3 7.3 %collective-permute-start.1 = (f32[16,4096]{1,0:T(8,128)S(1)}, f32[16,4096]{1,0:T(8,128)S(1)}, u32[]{:S(2)}, u32[]{:S(2)}) collective-permute-start(f32[16,4096]{1,0:T(8,128)S(1)} %pad_maximum_fusion.7), channel_id=1, source_target_pairs={{0,32},{4,228},{8,40},{12,236},{16,48},{20,244},{24,56},{28,252},{... | collective-permute-start | bytes 786440 | tf_op jit(solution)/shard_map/ppermute | solution.py:24
  13.3 6.1 %collective-permute-start.5 = (f32[16,4096]{1,0:T(8,128)S(1)}, f32[16,4096]{1,0:T(8,128)S(1)}, u32[]{:S(2)}, u32[]{:S(2)}) collective-permute-start(f32[16,4096]{1,0:T(8,128)S(1)} %pad_maximum_fusion.8), channel_id=1, source_target_pairs={{0,8},{4,28},{8,16},{12,4},{16,24},{20,12},{24,0},{28,20},{32,40},... | collective-permute-start | bytes 786440 | tf_op jit(solution)/shard_map/ppermute | solution.py:28
  16.6 45.8 %copy-start.1 = (f32[4096,256]{1,0:T(8,128)S(1)}, f32[4096,256]{1,0:T(8,128)}, u32[]{:S(2)}) copy-start(f32[4096,256]{1,0:T(8,128)} %param.9) | copy-start | bytes 12582916
  19.4 17.2 %collective-permute-start.6 = (f32[24,4096]{1,0:T(8,128)S(1)}, f32[24,4096]{1,0:T(8,128)}, u32[]{:S(2)}, u32[]{:S(2)}) collective-permute-start(f32[24,4096]{1,0:T(8,128)S(1)} %pad_maximum_fusion.5), channel_id=1, source_target_pairs={{0,8},{4,28},{8,16},{12,4},{16,24},{20,12},{24,0},{28,20},{32,40},... | collective-permute-start | bytes 1179656 | tf_op jit(solution)/shard_map/ppermute | solution.py:28
  22.5 5.2 %collective-permute-start.2 = (f32[16,4096]{1,0:T(8,128)S(1)}, f32[16,4096]{1,0:T(8,128)S(1)}, u32[]{:S(2)}, u32[]{:S(2)}) collective-permute-start(f32[16,4096]{1,0:T(8,128)S(1)} %collective-permute-done.1), channel_id=1, source_target_pairs={{0,32},{4,228},{8,40},{12,236},{16,48},{20,244},{24,56},{28,252},{... | collective-permute-start | bytes 786440 | tf_op jit(solution)/shard_map/ppermute | solution.py:24
  27.8 5.6 %collective-permute-start.3 = (f32[16,4096]{1,0:T(8,128)S(1)}, f32[16,4096]{1,0:T(8,128)S(1)}, u32[]{:S(2)}, u32[]{:S(2)}) collective-permute-start(f32[16,4096]{1,0:T(8,128)S(1)} %collective-permute-done.2), channel_id=1, source_target_pairs={{0,32},{4,228},{8,40},{12,236},{16,48},{20,244},{24,56},{28,252},{... | collective-permute-start | bytes 786440 | tf_op jit(solution)/shard_map/ppermute | solution.py:24
  33.4 5.1 %collective-permute-start.4 = (f32[8,4096]{1,0:T(8,128)S(1)}, f32[8,4096]{1,0:T(8,128)S(1)}, u32[]{:S(2)}, u32[]{:S(2)}) collective-permute-start(f32[8,4096]{1,0:T(8,128)S(1)} %constant_dynamic-slice_fusion.1), channel_id=1, source_target_pairs={{0,32},{4,228},{8,40},{12,236},{16,48},{20,244},{24,56},{28,252},{... | collective-permute-start | bytes 393224 | tf_op jit(solution)/shard_map/ppermute | solution.py:24
  36.6 25.8 %collective-permute-start.12 = (f32[1024,256]{1,0:T(8,128)S(1)}, f32[1024,256]{1,0:T(8,128)}, u32[]{:S(2)}, u32[]{:S(2)}) collective-permute-start(f32[1024,256]{1,0:T(8,128)S(1)} %get-tuple-element.19), channel_id=1, source_target_pairs={{0,4},{4,0},{8,12},{12,8},{16,20},{20,16},{24,28},{28,24},{32,36},... | collective-permute-start | bytes 3145736 | tf_op jit(solution)/shard_map/ppermute | solution.py:32
  38.6 9.8 %collective-permute-start.7 = (f32[40,4096]{1,0:T(8,128)S(1)}, f32[40,4096]{1,0:T(8,128)S(1)}, u32[]{:S(2)}, u32[]{:S(2)}) collective-permute-start(f32[40,4096]{1,0:T(8,128)S(1)} %pad_maximum_fusion.2), channel_id=1, source_target_pairs={{0,8},{4,28},{8,16},{12,4},{16,24},{20,12},{24,0},{28,20},{32,40},... | collective-permute-start | bytes 1966088 | tf_op jit(solution)/shard_map/ppermute | solution.py:28
  48.4 12.0 %copy-start.6 = (f32[40,4096]{1,0:T(8,128)}, f32[40,4096]{1,0:T(8,128)S(1)}, u32[]{:S(2)}) copy-start(f32[40,4096]{1,0:T(8,128)S(1)} %collective-permute-done.7) | copy-start | bytes 1966084
  48.4 4.1 %collective-permute-start.8 = (f32[8,4096]{1,0:T(8,128)S(1)}, f32[8,4096]{1,0:T(8,128)S(1)}, u32[]{:S(2)}, u32[]{:S(2)}) collective-permute-start(f32[8,4096]{1,0:T(8,128)S(1)} %constant_dynamic-slice_fusion), channel_id=1, source_target_pairs={{0,8},{4,28},{8,16},{12,4},{16,24},{20,12},{24,0},{28,20},{32,40},... | collective-permute-start | bytes 393224 | tf_op jit(solution)/shard_map/ppermute | solution.py:28
  49.4 11.0 %copy-start.2 = (f32[224,4096]{1,0:T(8,128)}, f32[224,4096]{1,0:T(8,128)S(1)}, u32[]{:S(2)}) copy-start(f32[224,4096]{1,0:T(8,128)S(1)} %get-tuple-element.70) | copy-start | bytes 11010052
  52.5 14.7 %collective-permute-start.16 = (f32[24,4096]{1,0:T(8,128)}, f32[24,4096]{1,0:T(8,128)}, u32[]{:S(2)}, u32[]{:S(2)}) collective-permute-start(f32[24,4096]{1,0:T(8,128)} %collective-permute-done.6), channel_id=1, source_target_pairs={{0,8},{4,28},{8,16},{12,4},{16,24},{20,12},{24,0},{28,20},{32,40},... | collective-permute-start | bytes 1179656 | tf_op jit(solution)/shard_map/ppermute | solution.py:28
  55.2 5.2 %copy-start.3 = (f32[1024,256]{1,0:T(8,128)}, f32[1024,256]{1,0:T(8,128)S(1)}, u32[]{:S(2)}) copy-start(f32[1024,256]{1,0:T(8,128)S(1)} %collective-permute-done.15) | copy-start | bytes 3145732
  55.2 16.0 %collective-permute-start.10 = (f32[32,4096]{1,0:T(8,128)}, f32[32,4096]{1,0:T(8,128)}, u32[]{:S(2)}, u32[]{:S(2)}) collective-permute-start(f32[32,4096]{1,0:T(8,128)} %pad_maximum_fusion.3), channel_id=1, source_target_pairs={{0,4},{4,0},{8,12},{12,8},{16,20},{20,16},{24,28},{28,24},{32,36},... | collective-permute-start | bytes 1572872 | tf_op jit(solution)/shard_map/ppermute | solution.py:32
  60.4 1.1 copy-start.4
  61.4 1.0 copy-start.5
  67.2 8.1 %collective-permute-start.23 = (f32[24,4096]{1,0:T(8,128)}, f32[24,4096]{1,0:T(8,128)S(1)}, u32[]{:S(2)}, u32[]{:S(2)}) collective-permute-start(f32[24,4096]{1,0:T(8,128)} %collective-permute-done.16), channel_id=1, source_target_pairs={{0,8},{4,28},{8,16},{12,4},{16,24},{20,12},{24,0},{28,20},{32,40},... | collective-permute-start | bytes 1179656 | tf_op jit(solution)/shard_map/ppermute | solution.py:28
  70.2 8.5 %collective-permute-start.9 = (f32[32,4096]{1,0:T(8,128)}, f32[32,4096]{1,0:T(8,128)S(1)}, u32[]{:S(2)}, u32[]{:S(2)}) collective-permute-start(f32[32,4096]{1,0:T(8,128)} %pad_maximum_fusion.3), channel_id=1, source_target_pairs={{0,32},{4,228},{8,40},{12,236},{16,48},{20,244},{24,56},{28,252},{... | collective-permute-start | bytes 1572872 | tf_op jit(solution)/shard_map/ppermute | solution.py:24
  70.2 28.7 %collective-permute-start.17 = (f32[40,4096]{1,0:T(8,128)}, f32[40,4096]{1,0:T(8,128)S(1)}, u32[]{:S(2)}, u32[]{:S(2)}) collective-permute-start(f32[40,4096]{1,0:T(8,128)} %copy-done.6), channel_id=1, source_target_pairs={{0,8},{4,28},{8,16},{12,4},{16,24},{20,12},{24,0},{28,20},{32,40},... | collective-permute-start | bytes 1966088 | tf_op jit(solution)/shard_map/ppermute | solution.py:28
  71.1 13.3 %collective-permute-start.11 = (f32[32,4096]{1,0:T(8,128)}, f32[32,4096]{1,0:T(8,128)S(1)}, u32[]{:S(2)}, u32[]{:S(2)}) collective-permute-start(f32[32,4096]{1,0:T(8,128)} %collective-permute-done.10), channel_id=1, source_target_pairs={{0,32},{4,228},{8,40},{12,236},{16,48},{20,244},{24,56},{28,252},{... | collective-permute-start | bytes 1572872 | tf_op jit(solution)/shard_map/ppermute | solution.py:24
  78.8 13.0 %collective-permute-start.18 = (f32[32,4096]{1,0:T(8,128)S(1)}, f32[32,4096]{1,0:T(8,128)S(1)}, u32[]{:S(2)}, u32[]{:S(2)}) collective-permute-start(f32[32,4096]{1,0:T(8,128)S(1)} %collective-permute-done.9), channel_id=1, source_target_pairs={{0,32},{4,228},{8,40},{12,236},{16,48},{20,244},{24,56},{28,252},{... | collective-permute-start | bytes 1572872 | tf_op jit(solution)/shard_map/ppermute | solution.py:24
  88.7 8.4 %collective-permute-start.19 = (f32[32,4096]{1,0:T(8,128)S(1)}, f32[32,4096]{1,0:T(8,128)S(1)}, u32[]{:S(2)}, u32[]{:S(2)}) collective-permute-start(f32[32,4096]{1,0:T(8,128)S(1)} %collective-permute-done.11), channel_id=1, source_target_pairs={{0,32},{4,228},{8,40},{12,236},{16,48},{20,244},{24,56},{28,252},{... | collective-permute-start | bytes 1572872 | tf_op jit(solution)/shard_map/ppermute | solution.py:24
  91.8 11.0 %collective-permute-start.25 = (f32[32,4096]{1,0:T(8,128)S(1)}, f32[32,4096]{1,0:T(8,128)S(1)}, u32[]{:S(2)}, u32[]{:S(2)}) collective-permute-start(f32[32,4096]{1,0:T(8,128)S(1)} %collective-permute-done.18), channel_id=1, source_target_pairs={{0,32},{4,228},{8,40},{12,236},{16,48},{20,244},{24,56},{28,252},{... | collective-permute-start | bytes 1572872 | tf_op jit(solution)/shard_map/ppermute | solution.py:24
  97.1 14.1 %collective-permute-start.26 = (f32[32,4096]{1,0:T(8,128)S(1)}, f32[32,4096]{1,0:T(8,128)S(1)}, u32[]{:S(2)}, u32[]{:S(2)}) collective-permute-start(f32[32,4096]{1,0:T(8,128)S(1)} %collective-permute-done.19), channel_id=1, source_target_pairs={{0,32},{4,228},{8,40},{12,236},{16,48},{20,244},{24,56},{28,252},{... | collective-permute-start | bytes 1572872 | tf_op jit(solution)/shard_map/ppermute | solution.py:24
  99.0 10.0 %collective-permute-start.24 = (f32[40,4096]{1,0:T(8,128)S(1)}, f32[40,4096]{1,0:T(8,128)S(1)}, u32[]{:S(2)}, u32[]{:S(2)}) collective-permute-start(f32[40,4096]{1,0:T(8,128)S(1)} %collective-permute-done.17), channel_id=1, source_target_pairs={{0,8},{4,28},{8,16},{12,4},{16,24},{20,12},{24,0},{28,20},{32,40},... | collective-permute-start | bytes 1966088 | tf_op jit(solution)/shard_map/ppermute | solution.py:28
  102.7 11.2 %collective-permute-start.27 = (f32[32,4096]{1,0:T(8,128)S(1)}, f32[32,4096]{1,0:T(8,128)S(1)}, u32[]{:S(2)}, u32[]{:S(2)}) collective-permute-start(f32[32,4096]{1,0:T(8,128)S(1)} %collective-permute-done.25), channel_id=1, source_target_pairs={{0,32},{4,228},{8,40},{12,236},{16,48},{20,244},{24,56},{28,252},{... | collective-permute-start | bytes 1572872 | tf_op jit(solution)/shard_map/ppermute | solution.py:24
  105.2 15.9 %collective-permute-start.20 = (f32[352,128]{1,0:T(8,128)S(1)}, f32[352,128]{1,0:T(8,128)S(1)}, u32[]{:S(2)}, u32[]{:S(2)}) collective-permute-start(f32[352,128]{1,0:T(8,128)S(1)} %get-tuple-element.41), channel_id=1, source_target_pairs={{0,1},{1,2},{2,3},{3,0},{4,5},{5,6},{6,7},{7,4},{8,9},{9,10},{10,1... | collective-permute-start | bytes 540680 | tf_op jit(solution)/shard_map/ppermute | solution.py:36
  106.5 15.8 %collective-permute-start.22 = (f32[352,128]{1,0:T(8,128)S(1)}, f32[352,128]{1,0:T(8,128)S(1)}, u32[]{:S(2)}, u32[]{:S(2)}) collective-permute-start(f32[352,128]{1,0:T(8,128)S(1)} %get-tuple-element.42), channel_id=1, source_target_pairs={{0,2},{1,3},{2,0},{3,1},{4,6},{5,7},{6,4},{7,5},{8,10},{9,11},{10,... | collective-permute-start | bytes 540680 | tf_op jit(solution)/shard_map/ppermute | solution.py:36
  108.9 13.3 %collective-permute-start.21 = (f32[352,128]{1,0:T(8,128)S(1)}, f32[352,128]{1,0:T(8,128)S(1)}, u32[]{:S(2)}, u32[]{:S(2)}) collective-permute-start(f32[352,128]{1,0:T(8,128)S(1)} %get-tuple-element.43), channel_id=1, source_target_pairs={{0,3},{1,0},{2,1},{3,2},{4,7},{5,4},{6,5},{7,6},{8,11},{9,8},{10,9... | collective-permute-start | bytes 540680 | tf_op jit(solution)/shard_map/ppermute | solution.py:36
  117.4 4.9 %collective-permute-start.28 = (f32[160,128]{1,0:T(8,128)S(1)}, f32[160,128]{1,0:T(8,128)S(1)}, u32[]{:S(2)}, u32[]{:S(2)}) collective-permute-start(f32[160,128]{1,0:T(8,128)S(1)} %get-tuple-element.57), channel_id=1, source_target_pairs={{0,1},{1,2},{2,3},{3,0},{4,5},{5,6},{6,7},{7,4},{8,9},{9,10},{10,1... | collective-permute-start | bytes 245768 | tf_op jit(solution)/shard_map/ppermute | solution.py:36
  118.7 5.1 %collective-permute-start.30 = (f32[160,128]{1,0:T(8,128)S(1)}, f32[160,128]{1,0:T(8,128)S(1)}, u32[]{:S(2)}, u32[]{:S(2)}) collective-permute-start(f32[160,128]{1,0:T(8,128)S(1)} %get-tuple-element.58), channel_id=1, source_target_pairs={{0,2},{1,3},{2,0},{3,1},{4,6},{5,7},{6,4},{7,5},{8,10},{9,11},{10,... | collective-permute-start | bytes 245768 | tf_op jit(solution)/shard_map/ppermute | solution.py:36
  121.1 3.6 %collective-permute-start.29 = (f32[160,128]{1,0:T(8,128)S(1)}, f32[160,128]{1,0:T(8,128)S(1)}, u32[]{:S(2)}, u32[]{:S(2)}) collective-permute-start(f32[160,128]{1,0:T(8,128)S(1)} %get-tuple-element.59), channel_id=1, source_target_pairs={{0,3},{1,0},{2,1},{3,2},{4,7},{5,4},{6,5},{7,6},{8,11},{9,8},{10,9... | collective-permute-start | bytes 245768 | tf_op jit(solution)/shard_map/ppermute | solution.py:36
  125.0 5.4 %collective-permute-start.31 = (f32[512,128]{1,0:T(8,128)S(1)}, f32[512,128]{1,0:T(8,128)S(1)}, u32[]{:S(2)}, u32[]{:S(2)}) collective-permute-start(f32[512,128]{1,0:T(8,128)S(1)} %fusion.20), channel_id=1, source_target_pairs={{0,4},{4,0},{8,12},{12,8},{16,20},{20,16},{24,28},{28,24},{32,36},... | collective-permute-start | bytes 786440 | tf_op jit(solution)/shard_map/ppermute | solution.py:32
